TPU v7x, 256 devices: a whole 4x4x8 slice. The times are simulated.
256 devices in a mesh: clip: 32 (over x, z_hi, core), tile: 8 (over y, z_lo).
Axes of the slice: x: 4, y: 4, z: 8 (z_hi: 4, z_lo: 2; z = z_hi * 2 + z_lo), core: 2. Of those that a mesh axis runs over, the one named last changes fastest.
Arguments:
- latents: bfloat16 [64, 40, 64, 320], P('clip', 'tile'), may hold values from -64 to 64
- lengths: int32 [32], P('clip'), may hold values from 1 to 2, as said below
- context: int32 [8], replicated, may hold values from 0 to 63, as said below
- gain_first: float32 [320], replicated, may hold values from 0.25 to 1.75
- conv_first: bfloat16 [3, 3, 320, 320], replicated, may hold values from -0.109375 to 0.109375
- gain_second: float32 [320], replicated, may hold values from 0.25 to 1.75
- conv_second: bfloat16 [3, 3, 320, 320], replicated, may hold values from -0.109375 to 0.109375
- time_weight: bfloat16 [3, 320, 320], replicated, may hold values from -0.1875 to 0.1875
- attn_gain: float32 [320], replicated, may hold values from 0.25 to 1.75
- w_qkv: bfloat16 [320, 960], replicated, may hold values from -2 to 2
- w_out: bfloat16 [320, 320], replicated, may hold values from -0.3125 to 0.3125
Outputs:
- block_out: bfloat16 [64, 40, 64, 320], P('clip', 'tile')
Inputs may be any that keep to these rules, and one draw needn't show every extreme that they name: `lengths`: the last clip is full with 2 live frames and some other clip has 1. The context frames lie in distinct clips; each names slot c * 2 + f of a live frame f < lengths[c].
All inputs are finite; a program needn't handle non-finite values.
Results may differ from a plain program's by a relative error of at most 0.011.
Values may be sent and summed in bfloat16 or wider, within the bound.
A program may use at most 64 MiB of HBM per device.

v0:
```python
import jax
import jax.numpy as jnp
from jax import lax
from jax.sharding import PartitionSpec as P

HEAD_DIM = 64
GROUPS = 32
H = 40
W = 64


EPS = 1e-05
MASKED = -1e30


def with_halo(block, sides, width):
    for axis, dim in sides:
        count = lax.axis_size(axis)
        forward = [(i, i + 1) for i in range(count - 1)]
        backward = [(target, source) for source, target in forward]
        low = lax.ppermute(
            lax.slice_in_dim(block, block.shape[dim] - width, None, axis=dim), axis, forward
        )
        high = lax.ppermute(lax.slice_in_dim(block, 0, width, axis=dim), axis, backward)
        block = jnp.concatenate([low, block, high], axis=dim)
    return block


def from_behind(block, axis, distance):
    devices = range(lax.axis_size(axis))
    route = [(i - distance, i) for i in devices if i - distance in devices]
    return lax.ppermute(block, axis, route)


def finish(total_sum, square_sum, gain):
    group_width = gain.shape[0] // GROUPS
    count = H * W * group_width
    centre = total_sum / count
    spread = square_sum / count - centre * centre
    inverse = lax.rsqrt(spread + EPS)
    scale = jnp.repeat(inverse, group_width, axis=1) * gain[None, :]
    shift = -jnp.repeat(centre, group_width, axis=1) * scale
    return (scale, shift)


def activate(source, scale, shift):
    return jax.nn.silu(
        source.astype(jnp.float32) * scale[:, None, None, :] + shift[:, None, None, :]
    ).astype(jnp.bfloat16)


def convolve(padded, weights):
    wide = jnp.pad(padded, ((0, 0), (0, 0), (1, 1), (0, 0)))
    row_count = padded.shape[1] - 2
    col_count = padded.shape[2]
    result = jnp.zeros((padded.shape[0], row_count, col_count, weights.shape[-1]), jnp.float32)
    for row_step in range(3):
        for col_step in range(3):
            window = wide[:, row_step : row_step + row_count, col_step : col_step + col_count, :]
            result = result + jnp.dot(
                window, weights[row_step, col_step], preferred_element_type=jnp.float32
            )
    return result


def conv_section(source, gain, weights):
    frame_count, tile_rows, col_count, channels = source.shape
    group_width = channels // GROUPS
    values = source.astype(jnp.float32).reshape(
        frame_count, tile_rows * col_count, GROUPS, group_width
    )
    total_sum, square_sum = lax.psum(
        (jnp.sum(values, axis=(1, 3)), jnp.sum(values * values, axis=(1, 3))), "tile"
    )
    scale, shift = finish(total_sum, square_sum, gain)
    activated = activate(source, scale, shift)
    padded = with_halo(activated, (("tile", 1),), 1)
    return convolve(padded, weights)


def layer_norm(source, gain):
    values = source.astype(jnp.float32)
    centre = jnp.mean(values, axis=-1, keepdims=True)
    spread = jnp.mean((values - centre) ** 2, axis=-1, keepdims=True)
    return ((values - centre) * lax.rsqrt(spread + EPS) * gain).astype(jnp.bfloat16)


def attend(packed, shared_kv, live_count):
    frame_count, cell_count, packed_width = packed.shape
    channels = packed_width // 3
    head_count = channels // HEAD_DIM
    shape_local = (frame_count, cell_count, head_count, HEAD_DIM)
    shape_shared = (shared_kv.shape[0], cell_count, head_count, HEAD_DIM)
    queries = packed[..., :channels].reshape(shape_local)
    keys_local = packed[..., channels : 2 * channels].reshape(shape_local)
    values_local = packed[..., 2 * channels :].reshape(shape_local)
    keys_shared = shared_kv[..., :channels].reshape(shape_shared)
    values_shared = shared_kv[..., channels:].reshape(shape_shared)
    score_scale = HEAD_DIM ** (-0.5)
    near_scores = (
        jnp.einsum("fnhd,gnhd->nhfg", queries, keys_local, preferred_element_type=jnp.float32)
        * score_scale
    )
    visible = jnp.arange(frame_count) < live_count
    near_scores = jnp.where(visible, near_scores, MASKED)
    far_scores = (
        jnp.einsum("fnhd,jnhd->nhfj", queries, keys_shared, preferred_element_type=jnp.float32)
        * score_scale
    )
    ceiling = jnp.maximum(jnp.max(near_scores, axis=-1), jnp.max(far_scores, axis=-1))[..., None]
    near_exp = jnp.exp(near_scores - ceiling)
    far_exp = jnp.exp(far_scores - ceiling)
    normaliser = jnp.sum(near_exp, axis=-1, keepdims=True) + jnp.sum(
        far_exp, axis=-1, keepdims=True
    )
    near_weight = (near_exp / normaliser).astype(jnp.bfloat16)
    far_weight = (far_exp / normaliser).astype(jnp.bfloat16)
    result = jnp.einsum(
        "nhfg,gnhd->fnhd", near_weight, values_local, preferred_element_type=jnp.float32
    )
    result = result + jnp.einsum(
        "nhfj,jnhd->fnhd", far_weight, values_shared, preferred_element_type=jnp.float32
    )
    return result.reshape(frame_count, cell_count, channels).astype(jnp.bfloat16)


def local(
    latents,
    lengths,
    context,
    gain_first,
    conv_first,
    gain_second,
    conv_second,
    time_weight,
    attn_gain,
    w_qkv,
    w_out,
):
    frame_count, tile_rows, col_count, channels = latents.shape
    hidden_one = conv_section(latents, gain_first, conv_first).astype(jnp.bfloat16)
    res_one = (
        latents.astype(jnp.float32) + conv_section(hidden_one, gain_second, conv_second)
    ).astype(jnp.bfloat16)
    moving = jax.nn.silu(res_one.astype(jnp.float32)).astype(jnp.bfloat16)
    live_count = lengths[0]
    final_frame = lax.dynamic_index_in_dim(moving, live_count - 1, 0, keepdims=False)
    prior = from_behind(final_frame, "clip", 1)
    later = from_behind(moving[0], "clip", -1)
    backward = jnp.concatenate([prior[None], moving[:-1]], axis=0)
    forward = jnp.concatenate([moving[1:], jnp.zeros_like(moving[:1])], axis=0)
    slots = jnp.arange(frame_count)
    forward = jnp.where((slots == live_count - 1)[:, None, None, None], later[None], forward)
    mixed = res_one.astype(jnp.float32) + jnp.dot(
        backward, time_weight[0], preferred_element_type=jnp.float32
    )
    mixed = mixed + jnp.dot(moving, time_weight[1], preferred_element_type=jnp.float32)
    mixed = mixed + jnp.dot(forward, time_weight[2], preferred_element_type=jnp.float32)
    res_two = mixed.astype(jnp.bfloat16)
    cell_count = tile_rows * col_count
    normed = layer_norm(res_two, attn_gain).reshape(frame_count, cell_count, channels)
    packed = jnp.dot(normed, w_qkv, preferred_element_type=jnp.float32).astype(jnp.bfloat16)
    selector = (context[:, None] == lax.axis_index("clip") * frame_count + slots[None, :]).astype(
        jnp.bfloat16
    )
    picked = jnp.einsum(
        "jf,fne->jne", selector, packed[..., channels:], preferred_element_type=jnp.float32
    )
    shared_kv = lax.psum(picked.astype(jnp.bfloat16), "clip")
    attended = attend(packed, shared_kv, live_count)
    result = res_two.astype(jnp.float32).reshape(frame_count, cell_count, channels)
    result = result + jnp.dot(attended, w_out, preferred_element_type=jnp.float32)
    result = jnp.where((slots < live_count)[:, None, None], result, 0.0)
    return result.astype(jnp.bfloat16).reshape(frame_count, tile_rows, col_count, channels)


def solution(mesh):
    placed = (P("clip", "tile", None, None), P("clip"), P(), P(), P(), P(), P(), P(), P(), P(), P())
    return jax.shard_map(
        local, mesh=mesh, in_specs=placed, out_specs=P("clip", "tile", None, None), check_vma=False
    )
```

profile of v0, /device:TPU:1, one launch (start us, length us, event | category | flops | bytes accessed | tf_op | source)
XLA Modules:
  0.0 459.4 jit_solution(14284970904354636011)
XLA Ops:
  8.2 17.6 %all-reduce.4 = (f32[2,32]{1,0:T(2,128)S(1)}, f32[2,32]{1,0:T(2,128)S(1)}) all-reduce(f32[2,32]{1,0:T(2,128)S(1)} %reduce_sum.105, f32[2,32]{1,0:T(2,128)S(1)} %reduce_sum.83), channel_id=1, replica_groups=mesh['clip'=32,'tile'=8] {'tile'}, use_global_device_ids=true, to_apply=%region_5.6 | all-reduce | flops 128 | bytes 1024 | tf_op jit(solution)/shard_map/psum | solution.py:72
  30.2 4.0 collective-permute-start
  42.0 14.3 %all-reduce.3 = (f32[2,32]{1,0:T(2,128)S(1)}, f32[2,32]{1,0:T(2,128)S(1)}) all-reduce(f32[2,32]{1,0:T(2,128)S(1)} %reduce_sum.111, f32[2,32]{1,0:T(2,128)S(1)} %reduce_sum.108), channel_id=1, replica_groups=mesh['clip'=32,'tile'=8] {'tile'}, use_global_device_ids=true, to_apply=%region_11.12 | all-reduce | flops 128 | bytes 1024 | tf_op jit(solution)/shard_map/psum | solution.py:72
  58.5 4.0 collective-permute-start.2
  70.4 15.7 %collective-permute-start.4 = (bf16[5,64,320]{2,1,0:T(8,128)(2,1)S(1)}, bf16[5,64,320]{2,1,0:T(8,128)(2,1)S(1)}, u32[]{:S(2)}, u32[]{:S(2)}) collective-permute-start(bf16[5,64,320]{2,1,0:T(8,128)(2,1)S(1)} %get-tuple-element.25), channel_id=1, source_target_pairs={{0,8},{8,16},{16,24},{24,32},{32,40},{40,48},{48,56},{56,64},{64,7... | collective-permute-start | bytes 614408 | tf_op jit(solution)/shard_map/ppermute | solution.py:32
  86.0 2.1 collective-permute-start.5
  89.6 7.2 %collective-permute-done.5 = bf16[5,64,320]{2,1,0:T(8,128)(2,1)S(1)} collective-permute-done((bf16[5,64,320]{2,1,0:T(8,128)(2,1)S(1)}, bf16[5,64,320]{2,1,0:T(8,128)(2,1)S(1)}, u32[]{:S(2)}, u32[]{:S(2)}) %collective-permute-start.5) | collective-permute-done | bytes 204832 | tf_op jit(solution)/shard_map/ppermute | solution.py:32
  99.4 3.1 convolution_convert_fusion
  105.0 1.9 copy.84
  107.1 1.9 copy.74
  109.3 1.9 copy.75
  111.2 3.2 fusion.141
  116.0 278.2 %all-reduce.7.cloned.1.call-done = bf16[8,320,640]{2,0,1:T(8,128)(2,1)} async-done(((bf16[8,320,640]{2,0,1:T(8,128)(2,1)}), bf16[8,320,640]{2,0,1:T(8,128)(2,1)}) %all-reduce.7.cloned.1.call-update) | async-done | bytes 3276816 | tf_op jit(solution)/shard_map/psum | solution.py:169
  394.2 5.2 %fusion.135 = (bf16[8,320,320]{2,0,1:T(8,128)(2,1)}, bf16[8,320,320]{2,0,1:T(8,128)(2,1)}) fusion(bf16[8,320,640]{2,0,1:T(8,128)(2,1)} %all-reduce.7.cloned.1.call-done), kind=kLoop, calls=%fused_computation.188 | loop fusion | bytes 6553600 | tf_op jit(solution)/shard_map/slice | solution.py:98
  399.4 4.1 copy.78
  403.5 5.5 %copy.80 = bf16[8,320,5,64]{3,0,2,1:T(8,128)(2,1)} copy(bf16[8,320,5,64]{1,3,2,0:T(8,128)(2,1)} %bitcast.194) | data formatting | bytes 3276800 | tf_op jit(solution)/shard_map/reshape | solution.py:97
  409.0 5.8 %fusion.140 = (f32[320,5,2]{2,1,0:T(8,128)S(1)}, f32[320,5,2,8]{3,2,1,0:T(2,128)}) fusion(bf16[2,320,5,64]{3,0,2,1:T(2,128)(2,1)} %copy.74, bf16[8,320,5,64]{3,0,2,1:T(8,128)(2,1)} %copy.80), kind=kOutput, calls=%fused_computation.193 | convolution fusion | flops 3324800 | bytes 2163200 | tf_op jit(solution)/shard_map/fnhd,jnhd->nhfj/dot_general | solution.py:107
  415.9 6.0 %fusion.31 = f32[320,5,2]{2,1,0:T(8,128)} fusion(f32[320,5,2,8]{3,2,1,0:T(2,128)} %get-tuple-element.40, f32[320,5,2]{2,1,0:T(8,128)S(1)} %copy.82), kind=kLoop, calls=%fused_computation.67 | loop fusion | flops 48000 | bytes 128000 | tf_op jit(solution)/shard_map/reduce_sum | solution.py:113
  425.2 1.9 copy.85
  427.1 4.1 copy.86
  431.2 5.5 %copy.88 = bf16[8,320,5,64]{3,0,2,1:T(8,128)(2,1)} copy(bf16[8,320,5,64]{1,3,2,0:T(8,128)(2,1)} %bitcast.195) | data formatting | bytes 3276800 | tf_op jit(solution)/shard_map/reshape | solution.py:98
  436.7 3.4 fusion.142
  440.1 8.7 %fusion.5 = bf16[2,320,5,64]{3,0,2,1:T(2,128)(2,1)} fusion(f32[320,5,64,2]{2,3,1,0:T(2,128)S(1)} %fusion.142, bf16[8,320,5,64]{3,0,2,1:T(8,128)(2,1)S(1)} %copy-done.2, f32[320,5,2,8]{3,2,1,0:T(2,128)S(1)} %copy-done.5, f32[320,5,2]{2,1,0:T(8,128)} %copy.87, f32[320,5,2]{2,1,0:T(8,128)S(1)} %copy.82), kind=kOutput, calls=%fused_computation.39 | convolution fusion | flops 3763200 | bytes 2995200 | tf_op jit(solution)/shard_map/nhfj,jnhd->fnhd/dot_general | solution.py:121
  448.9 2.3 copy.89
  (108 shorter events, 37.1 us)
Async XLA Ops:
  6.5 91.6 %copy-start = (bf16[320,960]{1,0:T(8,128)(2,1)S(1)}, bf16[320,960]{1,0:T(8,128)(2,1)}, u32[]{:S(2)}) copy-start(bf16[320,960]{1,0:T(8,128)(2,1)} %param.20) | copy-start | bytes 1843204
  6.5 387.7 %all-reduce.7.cloned.1.call-start = ((), (), s32[]{:S(2)}) async-start(), calls=%async_computation | async-start | bytes 6553600 | tf_op jit(solution)/shard_map/psum | solution.py:169
  7.8 28.6 %copy-start.4 = (bf16[3,3,320,320]{3,2,1,0:T(8,128)(2,1)S(1)}, bf16[3,3,320,320]{3,2,1,0:T(8,128)(2,1)}, u32[]{:S(2)}) copy-start(bf16[3,3,320,320]{3,2,1,0:T(8,128)(2,1)} %param.15) | copy-start | bytes 5529604
  28.9 6.5 %collective-permute-start.1 = (bf16[2,1,64,320]{3,2,1,0:T(8,128)(2,1)}, bf16[2,1,64,320]{3,2,1,0:T(8,128)(2,1)S(1)}, u32[]{:S(2)}, u32[]{:S(2)}) collective-permute-start(bf16[2,1,64,320]{3,2,1,0:T(8,128)(2,1)} %get-tuple-element.29), channel_id=1, source_target_pairs={{1,0},{2,1},{3,2},{4,3},{5,4},{6,5},{7,6},{9,8},{10,9},{11,10},{12... | collective-permute-start | bytes 245768 | tf_op jit(solution)/shard_map/ppermute | solution.py:24
  30.2 5.9 %collective-permute-start = (bf16[2,1,64,320]{3,2,1,0:T(8,128)(2,1)}, bf16[2,1,64,320]{3,2,1,0:T(8,128)(2,1)S(1)}, u32[]{:S(2)}, u32[]{:S(2)}) collective-permute-start(bf16[2,1,64,320]{3,2,1,0:T(8,128)(2,1)} %get-tuple-element.28), channel_id=1, source_target_pairs={{0,1},{1,2},{2,3},{3,4},{4,5},{5,6},{6,7},{8,9},{9,10},{10,11},{11... | collective-permute-start | bytes 245768 | tf_op jit(solution)/shard_map/ppermute | solution.py:21
  40.1 16.6 %copy-start.10 = (f32[320]{0:T(512)S(1)}, f32[320]{0:T(512)}, u32[]{:S(2)}) copy-start(f32[320]{0:T(512)} %param.16) | copy-start | bytes 3844
  57.0 8.7 %copy-start.6 = (bf16[3,3,320,320]{3,2,1,0:T(8,128)(2,1)S(1)}, bf16[3,3,320,320]{3,2,1,0:T(8,128)(2,1)}, u32[]{:S(2)}) copy-start(bf16[3,3,320,320]{3,2,1,0:T(8,128)(2,1)} %param.17) | copy-start | bytes 5529604
  57.0 5.5 %collective-permute-start.3 = (bf16[2,1,64,320]{3,2,1,0:T(8,128)(2,1)S(1)}, bf16[2,1,64,320]{3,2,1,0:T(8,128)(2,1)S(1)}, u32[]{:S(2)}, u32[]{:S(2)}) collective-permute-start(bf16[2,1,64,320]{3,2,1,0:T(8,128)(2,1)S(1)} %get-tuple-element.27), channel_id=1, source_target_pairs={{1,0},{2,1},{3,2},{4,3},{5,4},{6,5},{7,6},{9,8},{10,9},{11,10},{12... | collective-permute-start | bytes 245768 | tf_op jit(solution)/shard_map/ppermute | solution.py:24
  58.5 5.6 %collective-permute-start.2 = (bf16[2,1,64,320]{3,2,1,0:T(8,128)(2,1)S(1)}, bf16[2,1,64,320]{3,2,1,0:T(8,128)(2,1)S(1)}, u32[]{:S(2)}, u32[]{:S(2)}) collective-permute-start(bf16[2,1,64,320]{3,2,1,0:T(8,128)(2,1)S(1)} %get-tuple-element.26), channel_id=1, source_target_pairs={{0,1},{1,2},{2,3},{3,4},{4,5},{5,6},{6,7},{8,9},{9,10},{10,11},{11... | collective-permute-start | bytes 245768 | tf_op jit(solution)/shard_map/ppermute | solution.py:21
  68.5 1.0 copy-start.3
  70.2 17.9 %copy-start.7 = (bf16[3,320,320]{2,1,0:T(8,128)(2,1)S(1)}, bf16[3,320,320]{2,1,0:T(8,128)(2,1)}, u32[]{:S(2)}) copy-start(bf16[3,320,320]{2,1,0:T(8,128)(2,1)} %param.18) | copy-start | bytes 1843204
  70.4 18.8 %collective-permute-start.4 = (bf16[5,64,320]{2,1,0:T(8,128)(2,1)S(1)}, bf16[5,64,320]{2,1,0:T(8,128)(2,1)S(1)}, u32[]{:S(2)}, u32[]{:S(2)}) collective-permute-start(bf16[5,64,320]{2,1,0:T(8,128)(2,1)S(1)} %get-tuple-element.25), channel_id=1, source_target_pairs={{0,8},{8,16},{16,24},{24,32},{32,40},{40,48},{48,56},{56,64},{64,7... | collective-permute-start | bytes 614408 | tf_op jit(solution)/shard_map/ppermute | solution.py:32
  86.0 10.9 %collective-permute-start.5 = (bf16[5,64,320]{2,1,0:T(8,128)(2,1)S(1)}, bf16[5,64,320]{2,1,0:T(8,128)(2,1)S(1)}, u32[]{:S(2)}, u32[]{:S(2)}) collective-permute-start(bf16[5,64,320]{2,1,0:T(8,128)(2,1)S(1)} %get-tuple-element.22), channel_id=1, source_target_pairs={{8,0},{16,8},{24,16},{32,24},{40,32},{48,40},{56,48},{64,56},{72,6... | collective-permute-start | bytes 614408 | tf_op jit(solution)/shard_map/ppermute | solution.py:32
  88.6 8.3 %copy-start.12 = (pred[2]{0:T(512)(128)(4,1)S(1)}, pred[2]{0:T(512)(128)(4,1)}, u32[]{:S(2)}) copy-start(pred[2]{0:T(512)(128)(4,1)} %iota_compare_fusion.2) | copy-start | bytes 10
  96.9 0.9 copy-start.9
  98.1 1.3 copy-start.11
  436.7 3.4 copy-start.2
  436.7 3.4 copy-start.5
  440.1 11.1 %copy-start.8 = (bf16[320,320]{1,0:T(8,128)(2,1)S(1)}, bf16[320,320]{1,0:T(8,128)(2,1)}, u32[]{:S(2)}) copy-start(bf16[320,320]{1,0:T(8,128)(2,1)} %param.21) | copy-start | bytes 614404
  440.1 12.4 %copy-start.1 = (bf16[320,960]{1,0:T(8,128)(2,1)S(1)}, bf16[320,960]{1,0:T(8,128)(2,1)}, u32[]{:S(2)}) copy-start(bf16[320,960]{1,0:T(8,128)(2,1)} %param.20) | copy-start | bytes 1843204
Sparse Core Ops, SparseCore 0:
  102.7 291.5 all-reduce.6
where the time goes:
time: 463 us; the launch traced here: 459 us
  waiting for transfers between devices  288 us (62%)
  local copies, waits for them, and re-layouts  45.8 us (10%)
  matrix products  38.2 us (8%)
  blocking collectives  31.9 us (7%)
  starting transfers between devices  28.5 us (6%)
  between operations  14.6 us (3%)
  other arithmetic  12 us (3%)
    psum x1, waiting for transfers between devices, local(): shared_kv = lax.psum(picked.astype(jnp.bfloat16), 'clip')  278 us
    psum x2, blocking collectives, conv_section(): lax.psum((jnp.sum(values, axis=(1, 3)), jnp.sum(values * values, axis=(1,...  31.9 us
    ppermute x2, starting transfers between devices, from_behind(): return lax.ppermute(block, axis, route)  17.8 us
    dot_general x18, matrix products, convolve(): jnp.dot(window, weights[row_step, col_step], preferred_element_type=jnp.f...  10.4 us
    slice x2, local copies, waits for them, and re-layouts, attend(): values_shared = shared_kv[..., channels:].reshape(shape_shared)  9.27 us
  transfers between devices with their start and end apart: 7, of which 5 were waited for; matrix products, arithmetic and copies ran while one was open for 3% of the time, Pallas kernels for 0%

commit v1 on v0

v1 whole, which is shorter than its diff:
```python
import jax
import jax.numpy as jnp
from jax import lax
from jax.experimental import pallas as pl
from jax.experimental.pallas import tpu as pltpu
from jax.sharding import PartitionSpec as P

MESH = pl.DeviceIdType.MESH
F32 = jnp.float32
BF16 = jnp.bfloat16

C = 320
HEAD_DIM = 64
HEADS = 5
GROUP_WIDTH = 10
H = 40
W = 64
ROWS = 5
CLIPS = 32
TILES = 8
COUNT = H * W * GROUP_WIDTH
EPS = 1e-05
MASKED = -1e30
DEAD = 1e30
DEAD_LIMIT = 1e20
CHUNKS = ((0, 3), (3, 2))


def dot(a, b):
    return jnp.dot(a, b, preferred_element_type=F32)


def silu(y):
    half = 0.5 * y
    return half + half * jnp.tanh(half)


def rounded(v):
    return v.astype(BF16).astype(F32)


def channel_sums(frames):
    sums = [jnp.sum(v, axis=0, keepdims=True) for v in frames]
    squares = [jnp.sum(v * v, axis=0, keepdims=True) for v in frames]
    return jnp.concatenate(sums + squares + [jnp.zeros((4, C), F32)], axis=0)


def kernel(
    lat, length, context, gain_one, gain_two, gain_attn,
    w_one_hbm, w_two_hbm, w_time_hbm, w_qkv_hbm, w_out_hbm,
    out,
    w_one, w_two, w_time, w_qkv, w_out,
    taps, hid, halo, stat_send, stat_recv, packed, spread,
    send_0, send_1, recv_0, recv_1, back_send_0, back_send_1, back_recv_0, back_recv_1,
    load_sem, halo_send_sem, halo_recv_sem, stat_send_sem, stat_recv_sem,
    a2a_send_sem, a2a_recv_sem,
):
    clip = lax.axis_index("clip")
    tile = lax.axis_index("tile")
    tile_up = lax.rem(tile + TILES - 1, TILES)
    tile_down = lax.rem(tile + 1, TILES)

    barrier = pltpu.get_barrier_semaphore()

    def greet_tile(i, carry):
        pl.semaphore_signal(
            barrier, inc=1, device_id={"tile": lax.rem(tile + i, TILES)}, device_id_type=MESH
        )
        return carry

    def greet_clip(i, carry):
        pl.semaphore_signal(
            barrier, inc=1, device_id={"clip": lax.rem(clip + i, CLIPS)}, device_id_type=MESH
        )
        return carry

    lax.fori_loop(1, TILES, greet_tile, 0)
    lax.fori_loop(1, CLIPS, greet_clip, 0)

    loads = [
        pltpu.make_async_copy(source, target, load_sem.at[i])
        for i, (source, target) in enumerate(
            (
                (w_one_hbm, w_one),
                (w_two_hbm, w_two),
                (w_time_hbm, w_time),
                (w_qkv_hbm, w_qkv),
                (w_out_hbm, w_out),
            )
        )
    ]
    for load in loads:
        load.start()

    first = channel_sums([lat[0].astype(F32), lat[1].astype(F32)])
    stat_send[0] = first
    pl.semaphore_wait(barrier, TILES - 1 + CLIPS - 1)

    def halo_copies(phase, source):
        low = pltpu.make_async_remote_copy(
            src_ref=source.at[:, pl.ds((ROWS - 1) * W, W)],
            dst_ref=halo.at[phase, 0],
            send_sem=halo_send_sem.at[phase, 0],
            recv_sem=halo_recv_sem.at[phase, 0],
            device_id={"tile": tile_down},
            device_id_type=MESH,
        )
        high = pltpu.make_async_remote_copy(
            src_ref=source.at[:, pl.ds(0, W)],
            dst_ref=halo.at[phase, 1],
            send_sem=halo_send_sem.at[phase, 1],
            recv_sem=halo_recv_sem.at[phase, 1],
            device_id={"tile": tile_up},
            device_id_type=MESH,
        )
        return low, high

    def stat_copy(phase, peer, slot):
        return pltpu.make_async_remote_copy(
            src_ref=stat_send.at[phase],
            dst_ref=stat_recv.at[phase, slot],
            send_sem=stat_send_sem.at[phase, peer],
            recv_sem=stat_recv_sem.at[phase, slot],
            device_id={"tile": peer},
            device_id_type=MESH,
        )

    def exchange_start(phase, source):
        def send(i, carry):
            stat_copy(phase, lax.rem(tile + i, TILES), tile).start()
            return carry

        lax.fori_loop(1, TILES, send, 0)
        for copy in halo_copies(phase, source):
            copy.start()

    def exchange_finish(phase, source, own, gain):
        def arrive(i, carry):
            peer = lax.rem(tile + i, TILES)
            stat_copy(phase, peer, peer).wait_recv()
            return carry

        lax.fori_loop(1, TILES, arrive, 0)
        stat_recv[phase, tile] = own
        total = stat_recv[phase, 0]
        for i in range(1, TILES):
            total = total + stat_recv[phase, i]
        rows = lax.broadcasted_iota(jnp.int32, (C, C), 0)
        cols = lax.broadcasted_iota(jnp.int32, (C, C), 1)
        member = ((rows * 6554) >> 16) == ((cols * 6554) >> 16)
        grouped = jnp.dot(
            total,
            jnp.where(member, 1.0, 0.0).astype(F32),
            precision=lax.Precision.HIGHEST,
            preferred_element_type=F32,
        ) * (1.0 / COUNT)
        centre = grouped[0:2]
        variance = grouped[2:4] - centre * centre
        scale = lax.rsqrt(variance + EPS) * gain[...]
        shift = -centre * scale
        for copy in halo_copies(phase, source):
            copy.wait_recv()
        return scale, shift

    def exchange_drain(phase, source):
        def drain(i, carry):
            stat_copy(phase, lax.rem(tile + i, TILES), tile).wait_send()
            return carry

        lax.fori_loop(1, TILES, drain, 0)
        for copy in halo_copies(phase, source):
            copy.wait_send()

    def put_taps(f, start, rows, value, scale, shift, keep=None):
        a = silu(value.astype(F32) * scale + shift)
        if keep is not None:
            a = jnp.where(keep, a, 0.0)
        column = lax.broadcasted_iota(jnp.int32, (rows * W, C), 0) & (W - 1)
        before = jnp.where(column == 0, 0.0, pltpu.roll(a, 1, 0))
        after = jnp.where(column == W - 1, 0.0, pltpu.roll(a, rows * W - 1, 0))
        taps[f, pl.ds(start, rows * W), :] = jnp.concatenate(
            [before.astype(BF16), a.astype(BF16), after.astype(BF16)], axis=1
        )

    def fill_taps(phase, source, scale, shift):
        for f in range(2):
            sc, sh = scale[f : f + 1], shift[f : f + 1]
            put_taps(f, W, ROWS, source[f], sc, sh)
            put_taps(f, 0, 1, halo[phase, 0, f], sc, sh, tile > 0)
            put_taps(f, (ROWS + 1) * W, 1, halo[phase, 1, f], sc, sh, tile < TILES - 1)

    def convolve(f, row, rows, weights):
        total = dot(taps[f, pl.ds(row * W, rows * W), :], weights[0])
        for a in (1, 2):
            total = total + dot(taps[f, pl.ds((row + a) * W, rows * W), :], weights[a])
        return total

    exchange_start(0, lat)
    scale, shift = exchange_finish(0, lat, first, gain_one)
    fill_taps(0, lat, scale, shift)
    loads[0].wait()
    frames = []
    for f in range(2):
        value = convolve(f, 0, ROWS, w_one).astype(BF16)
        hid[f] = value
        frames.append(value.astype(F32))
    second = channel_sums(frames)
    stat_send[1] = second

    exchange_start(1, hid)
    exchange_drain(0, lat)
    scale, shift = exchange_finish(1, hid, second, gain_two)
    fill_taps(1, hid, scale, shift)
    loads[1].wait()

    def a2a_copy(way, chunk, source, target, peer, slot):
        return pltpu.make_async_remote_copy(
            src_ref=source.at[peer],
            dst_ref=target.at[slot],
            send_sem=a2a_send_sem.at[way, chunk, peer],
            recv_sem=a2a_recv_sem.at[way, chunk, slot],
            device_id={"clip": peer},
            device_id_type=MESH,
        )

    def pack_row(r, value):
        base = r * 10 * CLIPS
        packed[pl.ds(base, 128), :] = value[:, 0:128]
        packed[pl.ds(base + 128, 128), :] = value[:, 128:256]
        packed[pl.ds(base + 256, 64), :] = jnp.concatenate(
            [value[0:64, 256:320], value[64:128, 256:320]], axis=1
        )

    def a2a_start(way, chunk, source, target):
        row, rows = CHUNKS[chunk]
        depth = rows * 10

        def pick(peer):
            return packed[pl.ds(row * 10 * CLIPS + peer, depth, stride=CLIPS), :].astype(BF16)

        def stage(i, carry):
            peer = lax.rem(clip + i, CLIPS)
            source[peer] = pick(peer)
            return carry

        def send(i, carry):
            peer = lax.rem(clip + i, CLIPS)
            a2a_copy(way, chunk, source, target, peer, clip).start()
            return carry

        lax.fori_loop(1, CLIPS, stage, 0)
        target[clip] = pick(clip)
        lax.fori_loop(1, CLIPS, send, 0)

    def a2a_finish(way, chunk, source, target):
        rows = CHUNKS[chunk][1]
        depth = rows * 10

        def arrive(i, carry):
            peer = lax.rem(clip + i, CLIPS)
            a2a_copy(way, chunk, source, target, peer, peer).wait_recv()
            return carry

        lax.fori_loop(1, CLIPS, arrive, 0)

        def widen(i, carry):
            spread[pl.ds(pl.multiple_of(i * 32, 32), depth), :] = target[i].astype(F32)
            return carry

        lax.fori_loop(0, CLIPS, widen, 0)
        return [unpack_row(q) for q in range(rows)]

    def a2a_drain(way, chunk, source, target):
        def drain(i, carry):
            peer = lax.rem(clip + i, CLIPS)
            a2a_copy(way, chunk, source, target, peer, clip).wait_send()
            return carry

        lax.fori_loop(1, CLIPS, drain, 0)

    def unpack_row(q):
        def column(k):
            return spread[pl.ds(q * 10 + k, CLIPS, stride=32), :]

        left = jnp.concatenate([column(k) for k in range(4)], axis=0)
        middle = jnp.concatenate([column(4 + k) for k in range(4)], axis=0)
        tail = jnp.concatenate([column(8), column(9)], axis=0)
        right = jnp.concatenate([tail, pltpu.roll(tail, 64, 1)], axis=0)
        return jnp.concatenate([left, middle, right[:, 0:64]], axis=1)

    one_live = length[0] == 1
    sends, recvs = (send_0, send_1), (recv_0, recv_1)
    back_sends, back_recvs = (back_send_0, back_send_1), (back_recv_0, back_recv_1)

    for chunk, (row, rows) in enumerate(CHUNKS):
        halves = []
        for f in range(2):
            value = lat[f, pl.ds(row * W, rows * W), :].astype(F32) + convolve(f, row, rows, w_two)
            if f == 1:
                value = jnp.where(one_live, DEAD, value)
            halves.append(value)
        for q in range(rows):
            span = slice(q * W, (q + 1) * W)
            pack_row(row + q, jnp.concatenate([halves[0][span], halves[1][span]], axis=0))
        a2a_start(0, chunk, sends[chunk], recvs[chunk])

    for load in loads[2:]:
        load.wait()
    exchange_drain(1, hid)

    lane = lax.broadcasted_iota(jnp.int32, (128, 128), 1)
    line = lax.broadcasted_iota(jnp.int32, (128, 128), 0)
    lane_clip, lane_cell, lane_slot = lane & 31, (lane >> 5) & 1, lane >> 6
    line_clip, line_cell = line & 31, (line >> 5) & 1
    lane_frame = lane_clip * 2 + lane_slot
    shared = jnp.zeros((128, 128), F32)
    for j in range(8):
        shared = shared + jnp.where(lane_frame == context[j], 1.0, 0.0)
    low_half = lane < HEAD_DIM
    clip_row = lax.broadcasted_iota(jnp.int32, (CLIPS, C), 0)

    for chunk, (row, rows) in enumerate(CHUNKS):
        blocks = a2a_finish(0, chunk, sends[chunk], recvs[chunk])
        dead = jnp.broadcast_to(blocks[0][64:96, 0:1], (CLIPS, 128)) > DEAD_LIMIT
        dead_wide = jnp.broadcast_to(blocks[0][64:96, 0:1], (CLIPS, C)) > DEAD_LIMIT
        dead_f = jnp.where(dead, 1.0, 0.0)
        dead_lane = jnp.sum(
            jnp.where(
                lax.broadcasted_iota(jnp.int32, (CLIPS, 128), 0)
                == (lax.broadcasted_iota(jnp.int32, (CLIPS, 128), 1) & 31),
                dead_f,
                0.0,
            ),
            axis=0,
            keepdims=True,
        )
        live_key = 1.0 - jnp.where(lane_slot == 1, jnp.broadcast_to(dead_lane, (128, 128)), 0.0)
        weight = jnp.where(
            lane_cell == line_cell,
            jnp.where(lane_clip == line_clip, live_key, 0.0) + shared,
            0.0,
        )
        visible = weight > 0.0
        weight2 = jnp.concatenate([weight, weight], axis=1)
        visible2 = jnp.concatenate([visible, visible], axis=1)

        sources = []
        for q in range(rows):
            x = jnp.where(blocks[q] > DEAD_LIMIT, 0.0, blocks[q])
            sources.append(x)
            moving = rounded(silu(x))
            before, after = [None] * 4, [None] * 4
            for cell in range(2):
                m0 = moving[cell * 32 : cell * 32 + 32]
                m1 = moving[64 + cell * 32 : 96 + cell * 32]
                final = jnp.where(dead_wide, m0, m1)
                prior = jnp.where(clip_row == 0, 0.0, pltpu.roll(final, 1, 0))
                later = jnp.where(clip_row == CLIPS - 1, 0.0, pltpu.roll(m0, CLIPS - 1, 0))
                before[cell], before[2 + cell] = prior, m0
                after[cell], after[2 + cell] = jnp.where(dead_wide, later, m1), later
            taps[0, pl.ds(q * 128, 128), :] = jnp.concatenate(
                [
                    jnp.concatenate(before, axis=0).astype(BF16),
                    moving.astype(BF16),
                    jnp.concatenate(after, axis=0).astype(BF16),
                ],
                axis=1,
            )
        source = jnp.concatenate(sources, axis=0)
        res_two = rounded(source + dot(taps[0, pl.ds(0, rows * 128), :], w_time[...]))
        centre = jnp.mean(res_two, axis=1, keepdims=True)
        offset = res_two - centre
        variance = jnp.mean(offset * offset, axis=1, keepdims=True)
        normed = (offset * lax.rsqrt(variance + EPS) * gain_attn[...]).astype(BF16)
        q_all = dot(normed, w_qkv[:, 0:C]).astype(BF16)
        k_all = dot(normed, w_qkv[:, C : 2 * C]).astype(BF16)
        v_all = dot(normed, w_qkv[:, 2 * C : 3 * C]).astype(BF16)
        zero = jnp.zeros((128, 128), BF16)
        attended = []
        for q in range(rows):
            span = slice(q * 128, (q + 1) * 128)
            pieces = []
            for pair in range(2):
                cols = slice(pair * 128, (pair + 1) * 128)
                queries, keys, values = q_all[span, cols], k_all[span, cols], v_all[span, cols]
                keys2 = jnp.concatenate(
                    [jnp.where(low_half, keys, zero), jnp.where(low_half, zero, keys)], axis=0
                )
                values2 = jnp.concatenate(
                    [jnp.where(low_half, values, zero), jnp.where(low_half, zero, values)], axis=0
                )
                scores = lax.dot_general(
                    queries, keys2, (((1,), (1,)), ((), ())), preferred_element_type=F32
                ) * (HEAD_DIM**-0.5)
                scores = jnp.where(visible2, scores, MASKED)
                top = jnp.concatenate(
                    [
                        jnp.broadcast_to(
                            jnp.max(scores[:, i * 128 : (i + 1) * 128], axis=1, keepdims=True),
                            (128, 128),
                        )
                        for i in range(2)
                    ],
                    axis=1,
                )
                grown = jnp.exp(scores - top) * weight2
                norm = jnp.where(
                    low_half,
                    jnp.broadcast_to(jnp.sum(grown[:, 0:128], axis=1, keepdims=True), (128, 128)),
                    jnp.broadcast_to(jnp.sum(grown[:, 128:256], axis=1, keepdims=True), (128, 128)),
                )
                pieces.append((dot(grown.astype(BF16), values2) / norm).astype(BF16))
            cols = slice(256, 320)
            scores = lax.dot_general(
                q_all[span, cols], k_all[span, cols], (((1,), (1,)), ((), ())),
                preferred_element_type=F32,
            ) * (HEAD_DIM**-0.5)
            scores = jnp.where(visible, scores, MASKED)
            grown = jnp.exp(scores - jnp.max(scores, axis=1, keepdims=True)) * weight
            norm = jnp.sum(grown, axis=1, keepdims=True)
            pieces.append((dot(grown.astype(BF16), v_all[span, cols]) / norm).astype(BF16))
            attended.append(jnp.concatenate(pieces, axis=1))
        result = res_two + dot(jnp.concatenate(attended, axis=0), w_out[...])
        for q in range(rows):
            block = result[q * 128 : (q + 1) * 128]
            parts = [block[0:64]]
            for cell in range(2):
                parts.append(jnp.where(dead_wide, 0.0, block[64 + cell * 32 : 96 + cell * 32]))
            pack_row(row + q, jnp.concatenate(parts, axis=0))
        a2a_start(1, chunk, back_sends[chunk], back_recvs[chunk])

    for chunk in range(2):
        a2a_drain(0, chunk, sends[chunk], recvs[chunk])
    for chunk, (row, rows) in enumerate(CHUNKS):
        blocks = a2a_finish(1, chunk, back_sends[chunk], back_recvs[chunk])
        for q in range(rows):
            for f in range(2):
                out[f, pl.ds((row + q) * W, W), :] = blocks[q][f * 64 : (f + 1) * 64].astype(BF16)
    for chunk in range(2):
        a2a_drain(1, chunk, back_sends[chunk], back_recvs[chunk])


def local(
    latents, lengths, context, gain_first, conv_first, gain_second, conv_second,
    time_weight, attn_gain, w_qkv, w_out,
):
    vmem = pl.BlockSpec(memory_space=pltpu.VMEM)
    smem = pl.BlockSpec(memory_space=pltpu.SMEM)
    hbm = pl.BlockSpec(memory_space=pl.ANY)

    def messages(chunk):
        return pltpu.VMEM((CLIPS, CHUNKS[chunk][1] * 10, 128), BF16)

    result = pl.pallas_call(
        kernel,
        out_shape=jax.ShapeDtypeStruct((2, ROWS * W, C), BF16),
        in_specs=[vmem, smem, smem, vmem, vmem, vmem, hbm, hbm, hbm, hbm, hbm],
        out_specs=vmem,
        scratch_shapes=[
            pltpu.VMEM((3, 3 * C, C), BF16),
            pltpu.VMEM((3, 3 * C, C), BF16),
            pltpu.VMEM((3 * C, C), BF16),
            pltpu.VMEM((C, 3 * C), BF16),
            pltpu.VMEM((C, C), BF16),
            pltpu.VMEM((2, (ROWS + 2) * W, 3 * C), BF16),
            pltpu.VMEM((2, ROWS * W, C), BF16),
            pltpu.VMEM((2, 2, 2, W, C), BF16),
            pltpu.VMEM((2, 8, C), F32),
            pltpu.VMEM((2, TILES, 8, C), F32),
            pltpu.VMEM((ROWS * 10 * CLIPS, 128), F32),
            pltpu.VMEM((CLIPS * 32, 128), F32),
            messages(0), messages(1), messages(0), messages(1),
            messages(0), messages(1), messages(0), messages(1),
            pltpu.SemaphoreType.DMA((5,)),
            pltpu.SemaphoreType.DMA((2, 2)),
            pltpu.SemaphoreType.DMA((2, 2)),
            pltpu.SemaphoreType.DMA((2, TILES)),
            pltpu.SemaphoreType.DMA((2, TILES)),
            pltpu.SemaphoreType.DMA((2, 2, CLIPS)),
            pltpu.SemaphoreType.DMA((2, 2, CLIPS)),
        ],
        compiler_params=pltpu.CompilerParams(
            collective_id=0, has_side_effects=True, vmem_limit_bytes=48 << 20
        ),
        name="block",
    )(
        latents.reshape(2, ROWS * W, C),
        lengths,
        context,
        gain_first.reshape(1, C),
        gain_second.reshape(1, C),
        attn_gain.reshape(1, C),
        conv_first.reshape(3, 3 * C, C),
        conv_second.reshape(3, 3 * C, C),
        time_weight.reshape(3 * C, C),
        w_qkv,
        w_out,
    )
    return result.reshape(2, ROWS, W, C)


def solution(mesh):
    placed = (P("clip", "tile", None, None), P("clip"), P(), P(), P(), P(), P(), P(), P(), P(), P())
    return jax.shard_map(
        local, mesh=mesh, in_specs=placed, out_specs=P("clip", "tile", None, None), check_vma=False
    )
```

time: 463 us -> 73.7 us (0.16)
  waiting for transfers between devices: 288 us -> 0 us
  Pallas kernels: 0 us -> 63.4 us
  matrix products: 38.2 us -> 0 us
  local copies, waits for them, and re-layouts: 45.8 us -> 9.28 us
  blocking collectives: 31.9 us -> 0 us
  starting transfers between devices: 28.5 us -> 0 us
  between operations: 14.6 us -> 0.67 us
  other arithmetic: 12 us -> 0 us
    psum x1 -> x0, waiting for transfers between devices: 278 us -> none  [local(): shared_kv = lax.psum(picked.astype(jnp.bfloat16), 'clip')]
    pallas_call x0 -> x1, Pallas kernels: none -> 63.4 us  [local(): pl.pallas_call(kernel, out_shape=jax.ShapeDtypeStruct((2, ROWS * W, C), B...]
    dot_general x28 -> x0, matrix products: 38.2 us -> none  [the longest x18 10.4 us: convolve(): jnp.dot(window, weights[row_step, col_step], preferred_element_type=jnp.f...]
    psum x2 -> x0, blocking collectives: 31.9 us -> none  [conv_section(): lax.psum((jnp.sum(values, axis=(1, 3)), jnp.sum(values * values, axis=(1,...]
    ppermute x6 -> x0, starting transfers between devices: 28.5 us -> none  [the longest x2 17.8 us: from_behind(): return lax.ppermute(block, axis, route)]
    slice x10 -> x0, local copies, waits for them, and re-layouts: 17.5 us -> none  [the longest x2 9.27 us: attend(): values_shared = shared_kv[..., channels:].reshape(shape_shared)]
    reshape x7 -> x3, local copies, waits for them, and re-layouts: 17 us -> 2.05 us  [the longest x1 0.68 us: local(): gain_first.reshape(1, C)]
    ppermute x6 -> x0, waiting for transfers between devices: 10.2 us -> none  [the longest x2 7.79 us: from_behind(): return lax.ppermute(block, axis, route)]
  transfers between devices with their start and end apart: 7 -> 0, of which waited for: 5 -> 0; matrix products, arithmetic and copies ran while one was open for 3% -> 0% of each run, Pallas kernels for 0% -> 0%
where the time goes in v1:
time: 73.7 us; the launch traced here: 73.3 us
  Pallas kernels  63.4 us (86%)
  local copies, waits for them, and re-layouts  9.28 us (13%)
    pallas_call x1, Pallas kernels, local(): pl.pallas_call(kernel, out_shape=jax.ShapeDtypeStruct((2, ROWS * W, C), B...  63.4 us
    unnamed x13, local copies, waits for them, and re-layouts  7.23 us

profile of v1, /device:TPU:1, one launch (start us, length us, event | category | flops | bytes accessed | tf_op | source)
XLA Modules:
  0.0 73.3 jit_solution(16496082718251024376)
XLA Ops:
  0.7 0.7 reshape.25.gain_one
  1.3 0.7 reshape.26.gain_two
  2.0 0.7 reshape.27.gain_attn
  2.7 0.0 copy-start
  2.7 1.6 %copy-done = bf16[3,3,320,320]{3,2,1,0:T(8,128)(2,1)S(1)} copy-done((bf16[3,3,320,320]{3,2,1,0:T(8,128)(2,1)S(1)}, bf16[3,3,320,320]{3,2,1,0:T(8,128)(2,1)}, u32[]{:S(2)}) %copy-start) | copy-done | bytes 1843224
  4.3 0.0 copy-start.1
  4.3 1.1 %copy-done.1 = bf16[3,320,320]{2,1,0:T(8,128)(2,1)S(1)} copy-done((bf16[3,320,320]{2,1,0:T(8,128)(2,1)S(1)}, bf16[3,320,320]{2,1,0:T(8,128)(2,1)}, u32[]{:S(2)}) %copy-start.1) | copy-done | bytes 614424
  5.4 0.0 copy-start.2
  5.4 1.1 %copy-done.2 = bf16[320,960]{1,0:T(8,128)(2,1)S(1)} copy-done((bf16[320,960]{1,0:T(8,128)(2,1)S(1)}, bf16[320,960]{1,0:T(8,128)(2,1)}, u32[]{:S(2)}) %copy-start.2) | copy-done | bytes 614424
  6.5 0.0 copy-start.3
  6.5 1.0 %copy-done.3 = bf16[2,5,64,320]{3,2,1,0:T(8,128)(2,1)S(1)} copy-done((bf16[2,5,64,320]{3,2,1,0:T(8,128)(2,1)S(1)}, bf16[2,5,64,320]{3,2,1,0:T(8,128)(2,1)}, u32[]{:S(2)}) %copy-start.3) | copy-done | bytes 409624
  7.6 0.0 copy-start.4
  7.6 0.9 %copy-done.4 = bf16[320,320]{1,0:T(8,128)(2,1)S(1)} copy-done((bf16[320,320]{1,0:T(8,128)(2,1)S(1)}, bf16[320,320]{1,0:T(8,128)(2,1)}, u32[]{:S(2)}) %copy-start.4) | copy-done | bytes 204824
  8.5 0.0 copy-start.5
  8.5 0.7 copy-done.5
  9.2 63.4 %block.1 = bf16[2,320,320]{2,1,0:T(8,128)(2,1)S(1)} custom-call(bf16[2,320,320]{2,1,0:T(8,128)(2,1)S(1)} %bitcast.8, s32[1]{0:T(128)S(6)} %copy.13.length, s32[8]{0:T(128)S(1)} %copy-done.5, f32[1,320]{1,0:T(1,128)S(1)} %reshape.25.gain_one, f32[1,320]{1,0:T(1,128)S(1)} %reshape.26.gain_two, f32[1,320]{1,0:T(1,128)S(1)} %reshape.27.gain_attn, ...), custom_call_target="tpu_custom_call" | custom-call | tf_op jit(solution)/shard_map/block/pallas_call | solution.py:454
  72.6 0.8 %copy.14 = bf16[2,5,64,320]{3,2,1,0:T(8,128)(2,1)} copy(bf16[2,5,64,320]{3,2,1,0:T(8,128)(2,1)S(1)} %bitcast.6) | data formatting | bytes 819200
Async XLA Ops:
  2.7 1.6 %copy-start = (bf16[3,3,320,320]{3,2,1,0:T(8,128)(2,1)S(1)}, bf16[3,3,320,320]{3,2,1,0:T(8,128)(2,1)}, u32[]{:S(2)}) copy-start(bf16[3,3,320,320]{3,2,1,0:T(8,128)(2,1)} %param.15) | copy-start | bytes 5529604
  4.3 1.1 %copy-start.1 = (bf16[3,320,320]{2,1,0:T(8,128)(2,1)S(1)}, bf16[3,320,320]{2,1,0:T(8,128)(2,1)}, u32[]{:S(2)}) copy-start(bf16[3,320,320]{2,1,0:T(8,128)(2,1)} %param.18) | copy-start | bytes 1843204
  5.4 1.1 %copy-start.2 = (bf16[320,960]{1,0:T(8,128)(2,1)S(1)}, bf16[320,960]{1,0:T(8,128)(2,1)}, u32[]{:S(2)}) copy-start(bf16[320,960]{1,0:T(8,128)(2,1)} %w_qkv_hbm.1) | copy-start | bytes 1843204
  6.5 1.0 %copy-start.3 = (bf16[2,5,64,320]{3,2,1,0:T(8,128)(2,1)S(1)}, bf16[2,5,64,320]{3,2,1,0:T(8,128)(2,1)}, u32[]{:S(2)}) copy-start(bf16[2,5,64,320]{3,2,1,0:T(8,128)(2,1)} %param.11) | copy-start | bytes 1228804
  7.6 0.9 %copy-start.4 = (bf16[320,320]{1,0:T(8,128)(2,1)S(1)}, bf16[320,320]{1,0:T(8,128)(2,1)}, u32[]{:S(2)}) copy-start(bf16[320,320]{1,0:T(8,128)(2,1)} %w_out_hbm.1) | copy-start | bytes 614404
  8.5 0.7 copy-start.5

commit v2 on v1

--- a/solution.py
+++ b/solution.py
@@ -46,10 +46,10 @@
 
 
 def kernel(
-    lat, length, context, gain_one, gain_two, gain_attn,
+    lat_hbm, length, context, gain_one, gain_two, gain_attn,
     w_one_hbm, w_two_hbm, w_time_hbm, w_qkv_hbm, w_out_hbm,
     out,
-    w_one, w_two, w_time, w_qkv, w_out,
+    lat, w_one, w_two, w_time, w_qkv, w_out,
     taps, hid, halo, stat_send, stat_recv, packed, spread,
     send_0, send_1, recv_0, recv_1, back_send_0, back_send_1, back_recv_0, back_recv_1,
     load_sem, halo_send_sem, halo_recv_sem, stat_send_sem, stat_recv_sem,
@@ -60,27 +60,11 @@
     tile_up = lax.rem(tile + TILES - 1, TILES)
     tile_down = lax.rem(tile + 1, TILES)
 
-    barrier = pltpu.get_barrier_semaphore()
-
-    def greet_tile(i, carry):
-        pl.semaphore_signal(
-            barrier, inc=1, device_id={"tile": lax.rem(tile + i, TILES)}, device_id_type=MESH
-        )
-        return carry
-
-    def greet_clip(i, carry):
-        pl.semaphore_signal(
-            barrier, inc=1, device_id={"clip": lax.rem(clip + i, CLIPS)}, device_id_type=MESH
-        )
-        return carry
-
-    lax.fori_loop(1, TILES, greet_tile, 0)
-    lax.fori_loop(1, CLIPS, greet_clip, 0)
-
     loads = [
         pltpu.make_async_copy(source, target, load_sem.at[i])
         for i, (source, target) in enumerate(
             (
+                (lat_hbm, lat),
                 (w_one_hbm, w_one),
                 (w_two_hbm, w_two),
                 (w_time_hbm, w_time),
@@ -92,6 +76,24 @@
     for load in loads:
         load.start()
 
+    barrier = pltpu.get_barrier_semaphore()
+
+    def greet_tile(i, carry):
+        pl.semaphore_signal(
+            barrier, inc=1, device_id={"tile": lax.rem(tile + i, TILES)}, device_id_type=MESH
+        )
+        return carry
+
+    def greet_clip(i, carry):
+        pl.semaphore_signal(
+            barrier, inc=1, device_id={"clip": lax.rem(clip + i, CLIPS)}, device_id_type=MESH
+        )
+        return carry
+
+    lax.fori_loop(1, TILES, greet_tile, 0)
+    lax.fori_loop(1, CLIPS, greet_clip, 0)
+
+    loads[0].wait()
     first = channel_sums([lat[0].astype(F32), lat[1].astype(F32)])
     stat_send[0] = first
     pl.semaphore_wait(barrier, TILES - 1 + CLIPS - 1)
@@ -156,7 +158,7 @@
         ) * (1.0 / COUNT)
         centre = grouped[0:2]
         variance = grouped[2:4] - centre * centre
-        scale = lax.rsqrt(variance + EPS) * gain[...]
+        scale = lax.rsqrt(variance + EPS) * gain[...].reshape(1, C)
         shift = -centre * scale
         for copy in halo_copies(phase, source):
             copy.wait_recv()
@@ -198,7 +200,7 @@
     exchange_start(0, lat)
     scale, shift = exchange_finish(0, lat, first, gain_one)
     fill_taps(0, lat, scale, shift)
-    loads[0].wait()
+    loads[1].wait()
     frames = []
     for f in range(2):
         value = convolve(f, 0, ROWS, w_one).astype(BF16)
@@ -211,7 +213,7 @@
     exchange_drain(0, lat)
     scale, shift = exchange_finish(1, hid, second, gain_two)
     fill_taps(1, hid, scale, shift)
-    loads[1].wait()
+    loads[2].wait()
 
     def a2a_copy(way, chunk, source, target, peer, slot):
         return pltpu.make_async_remote_copy(
@@ -304,7 +306,7 @@
             pack_row(row + q, jnp.concatenate([halves[0][span], halves[1][span]], axis=0))
         a2a_start(0, chunk, sends[chunk], recvs[chunk])
 
-    for load in loads[2:]:
+    for load in loads[3:]:
         load.wait()
     exchange_drain(1, hid)
 
@@ -371,7 +373,7 @@
         centre = jnp.mean(res_two, axis=1, keepdims=True)
         offset = res_two - centre
         variance = jnp.mean(offset * offset, axis=1, keepdims=True)
-        normed = (offset * lax.rsqrt(variance + EPS) * gain_attn[...]).astype(BF16)
+        normed = (offset * lax.rsqrt(variance + EPS) * gain_attn[...].reshape(1, C)).astype(BF16)
         q_all = dot(normed, w_qkv[:, 0:C]).astype(BF16)
         k_all = dot(normed, w_qkv[:, C : 2 * C]).astype(BF16)
         v_all = dot(normed, w_qkv[:, 2 * C : 3 * C]).astype(BF16)
@@ -454,9 +456,10 @@
     result = pl.pallas_call(
         kernel,
         out_shape=jax.ShapeDtypeStruct((2, ROWS * W, C), BF16),
-        in_specs=[vmem, smem, smem, vmem, vmem, vmem, hbm, hbm, hbm, hbm, hbm],
+        in_specs=[hbm, smem, smem, vmem, vmem, vmem, hbm, hbm, hbm, hbm, hbm],
         out_specs=vmem,
         scratch_shapes=[
+            pltpu.VMEM((2, ROWS * W, C), BF16),
             pltpu.VMEM((3, 3 * C, C), BF16),
             pltpu.VMEM((3, 3 * C, C), BF16),
             pltpu.VMEM((3 * C, C), BF16),
@@ -471,7 +474,7 @@
             pltpu.VMEM((CLIPS * 32, 128), F32),
             messages(0), messages(1), messages(0), messages(1),
             messages(0), messages(1), messages(0), messages(1),
-            pltpu.SemaphoreType.DMA((5,)),
+            pltpu.SemaphoreType.DMA((6,)),
             pltpu.SemaphoreType.DMA((2, 2)),
             pltpu.SemaphoreType.DMA((2, 2)),
             pltpu.SemaphoreType.DMA((2, TILES)),
@@ -480,16 +483,16 @@
             pltpu.SemaphoreType.DMA((2, 2, CLIPS)),
         ],
         compiler_params=pltpu.CompilerParams(
-            collective_id=0, has_side_effects=True, vmem_limit_bytes=48 << 20
+            collective_id=0, has_side_effects=True, vmem_limit_bytes=67043328
         ),
         name="block",
     )(
         latents.reshape(2, ROWS * W, C),
         lengths,
         context,
-        gain_first.reshape(1, C),
-        gain_second.reshape(1, C),
-        attn_gain.reshape(1, C),
+        gain_first,
+        gain_second,
+        attn_gain,
         conv_first.reshape(3, 3 * C, C),
         conv_second.reshape(3, 3 * C, C),
         time_weight.reshape(3 * C, C),

time: 73.7 us -> 67.1 us (0.910)
  local copies, waits for them, and re-layouts: 9.28 us -> 1.86 us
  Pallas kernels: 63.4 us -> 64.4 us
    unnamed x13 -> x1, local copies, waits for them, and re-layouts: 7.23 us -> 1.86 us
    reshape x3 -> x0, local copies, waits for them, and re-layouts: 2.05 us -> none  [the longest x1 0.68 us: local(): gain_first.reshape(1, C)]
    pallas_call x1, Pallas kernels: 63.4 us -> 64.4 us  [local(): pl.pallas_call(kernel, out_shape=jax.ShapeDtypeStruct((2, ROWS * W, C), B...]
where the time goes in v2:
time: 67.1 us; the launch traced here: 67 us
  Pallas kernels  64.4 us (96%)
  local copies, waits for them, and re-layouts  1.86 us (3%)
    pallas_call x1, Pallas kernels, local(): pl.pallas_call(kernel, out_shape=jax.ShapeDtypeStruct((2, ROWS * W, C), B...  64.4 us
    unnamed x1, local copies, waits for them, and re-layouts  1.86 us

profile of v2, /device:TPU:1, one launch (start us, length us, event | category | flops | bytes accessed | tf_op | source)
XLA Modules:
  0.0 67.0 jit_solution(1190908769200954157)
XLA Ops:
  0.7 64.4 %block.1 = bf16[2,320,320]{2,1,0:T(8,128)(2,1)} custom-call(bf16[2,320,320]{2,1,0:T(8,128)(2,1)} %bitcast.9, s32[1]{0:T(128)S(6)} %copy.13.length, s32[8]{0:T(128)} %context.1, f32[320]{0:T(512)} %gain_one.1, f32[320]{0:T(512)} %gain_two.1, f32[320]{0:T(512)} %gain_attn.1, bf16[3,960,320]{2,1,0:T(8,128)(2,1)} %bitcast.5, bf16[3,960,320]{2,1,0:T(8,128)(2,1)} %bitcast.6, ...), custom_call_target="tpu_custom_call" | custom-call | tf_op jit(solution)/shard_map/block/pallas_call | solution.py:456
  65.1 1.9 %copy.14 = bf16[2,5,64,320]{3,2,1,0:T(8,128)(2,1)} copy(bf16[2,5,64,320]{3,2,1,0:T(8,128)(2,1)} %bitcast.7) | data formatting | bytes 819200

commit v3 on v2

--- a/solution.py
+++ b/solution.py
@@ -23,7 +23,8 @@
 MASKED = -1e30
 DEAD = 1e30
 DEAD_LIMIT = 1e20
-CHUNKS = ((0, 3), (3, 2))
+CHUNKS = ((1, 2, 3), (0, 4))
+STARTS = (0, 3)
 
 
 def dot(a, b):
@@ -42,7 +43,7 @@
 def channel_sums(frames):
     sums = [jnp.sum(v, axis=0, keepdims=True) for v in frames]
     squares = [jnp.sum(v * v, axis=0, keepdims=True) for v in frames]
-    return jnp.concatenate(sums + squares + [jnp.zeros((4, C), F32)], axis=0)
+    return jnp.concatenate(sums + squares, axis=0)
 
 
 def kernel(
@@ -50,7 +51,7 @@
     w_one_hbm, w_two_hbm, w_time_hbm, w_qkv_hbm, w_out_hbm,
     out,
     lat, w_one, w_two, w_time, w_qkv, w_out,
-    taps, hid, halo, stat_send, stat_recv, packed, spread,
+    taps, hid, halo_send, halo, member, stat_send, stat_recv, packed, spread,
     send_0, send_1, recv_0, recv_1, back_send_0, back_send_1, back_recv_0, back_recv_1,
     load_sem, halo_send_sem, halo_recv_sem, stat_send_sem, stat_recv_sem,
     a2a_send_sem, a2a_recv_sem,
@@ -93,29 +94,38 @@
     lax.fori_loop(1, TILES, greet_tile, 0)
     lax.fori_loop(1, CLIPS, greet_clip, 0)
 
+    rows = lax.broadcasted_iota(jnp.int32, (C, C), 0)
+    cols = lax.broadcasted_iota(jnp.int32, (C, C), 1)
+    member[...] = jnp.where(((rows * 6554) >> 16) == ((cols * 6554) >> 16), 1.0, 0.0).astype(BF16)
+
+    def pack_halo(phase, source):
+        for way, start in enumerate(((ROWS - 1) * W, 0)):
+            span = pl.ds(start, W)
+            for f in range(2):
+                halo_send[phase, way, 2 * f] = source[f, span, 0:128]
+                halo_send[phase, way, 2 * f + 1] = source[f, span, 128:256]
+            halo_send[phase, way, 4] = jnp.concatenate(
+                [source[0, span, 256:320], source[1, span, 256:320]], axis=1
+            )
+
     loads[0].wait()
+    pack_halo(0, lat)
     first = channel_sums([lat[0].astype(F32), lat[1].astype(F32)])
     stat_send[0] = first
     pl.semaphore_wait(barrier, TILES - 1 + CLIPS - 1)
 
-    def halo_copies(phase, source):
-        low = pltpu.make_async_remote_copy(
-            src_ref=source.at[:, pl.ds((ROWS - 1) * W, W)],
-            dst_ref=halo.at[phase, 0],
-            send_sem=halo_send_sem.at[phase, 0],
-            recv_sem=halo_recv_sem.at[phase, 0],
-            device_id={"tile": tile_down},
-            device_id_type=MESH,
-        )
-        high = pltpu.make_async_remote_copy(
-            src_ref=source.at[:, pl.ds(0, W)],
-            dst_ref=halo.at[phase, 1],
-            send_sem=halo_send_sem.at[phase, 1],
-            recv_sem=halo_recv_sem.at[phase, 1],
-            device_id={"tile": tile_up},
-            device_id_type=MESH,
-        )
-        return low, high
+    def halo_copies(phase):
+        return [
+            pltpu.make_async_remote_copy(
+                src_ref=halo_send.at[phase, way],
+                dst_ref=halo.at[phase, way],
+                send_sem=halo_send_sem.at[phase, way],
+                recv_sem=halo_recv_sem.at[phase, way],
+                device_id={"tile": peer},
+                device_id_type=MESH,
+            )
+            for way, peer in enumerate((tile_down, tile_up))
+        ]
 
     def stat_copy(phase, peer, slot):
         return pltpu.make_async_remote_copy(
@@ -127,50 +137,51 @@
             device_id_type=MESH,
         )
 
-    def exchange_start(phase, source):
+    def stats_start(phase):
         def send(i, carry):
             stat_copy(phase, lax.rem(tile + i, TILES), tile).start()
             return carry
 
         lax.fori_loop(1, TILES, send, 0)
-        for copy in halo_copies(phase, source):
+
+    def halo_start(phase):
+        for copy in halo_copies(phase):
             copy.start()
 
-    def exchange_finish(phase, source, own, gain):
+    def halo_finish(phase):
+        for copy in halo_copies(phase):
+            copy.wait_recv()
+
+    def stats_finish(phase, own, gain):
+        stat_recv[phase, tile] = own
+
         def arrive(i, carry):
             peer = lax.rem(tile + i, TILES)
             stat_copy(phase, peer, peer).wait_recv()
             return carry
 
         lax.fori_loop(1, TILES, arrive, 0)
-        stat_recv[phase, tile] = own
         total = stat_recv[phase, 0]
         for i in range(1, TILES):
             total = total + stat_recv[phase, i]
-        rows = lax.broadcasted_iota(jnp.int32, (C, C), 0)
-        cols = lax.broadcasted_iota(jnp.int32, (C, C), 1)
-        member = ((rows * 6554) >> 16) == ((cols * 6554) >> 16)
-        grouped = jnp.dot(
-            total,
-            jnp.where(member, 1.0, 0.0).astype(F32),
-            precision=lax.Precision.HIGHEST,
-            preferred_element_type=F32,
-        ) * (1.0 / COUNT)
+        top = total.astype(BF16)
+        rest = total - top.astype(F32)
+        mid = rest.astype(BF16)
+        low = (rest - mid.astype(F32)).astype(BF16)
+        grouped = dot(jnp.concatenate([top, mid, low], axis=0), member[...])
+        grouped = ((grouped[8:12] + grouped[4:8]) + grouped[0:4]) * (1.0 / COUNT)
         centre = grouped[0:2]
         variance = grouped[2:4] - centre * centre
         scale = lax.rsqrt(variance + EPS) * gain[...].reshape(1, C)
-        shift = -centre * scale
-        for copy in halo_copies(phase, source):
-            copy.wait_recv()
-        return scale, shift
-
-    def exchange_drain(phase, source):
+        return scale, -centre * scale
+
+    def exchange_drain(phase):
         def drain(i, carry):
             stat_copy(phase, lax.rem(tile + i, TILES), tile).wait_send()
             return carry
 
         lax.fori_loop(1, TILES, drain, 0)
-        for copy in halo_copies(phase, source):
+        for copy in halo_copies(phase):
             copy.wait_send()
 
     def put_taps(f, start, rows, value, scale, shift, keep=None):
@@ -184,36 +195,63 @@
             [before.astype(BF16), a.astype(BF16), after.astype(BF16)], axis=1
         )
 
-    def fill_taps(phase, source, scale, shift):
+    def fill_own(source, scale, shift):
         for f in range(2):
-            sc, sh = scale[f : f + 1], shift[f : f + 1]
-            put_taps(f, W, ROWS, source[f], sc, sh)
-            put_taps(f, 0, 1, halo[phase, 0, f], sc, sh, tile > 0)
-            put_taps(f, (ROWS + 1) * W, 1, halo[phase, 1, f], sc, sh, tile < TILES - 1)
-
-    def convolve(f, row, rows, weights):
-        total = dot(taps[f, pl.ds(row * W, rows * W), :], weights[0])
-        for a in (1, 2):
-            total = total + dot(taps[f, pl.ds((row + a) * W, rows * W), :], weights[a])
+            put_taps(f, W, ROWS, source[f], scale[f : f + 1], shift[f : f + 1])
+
+    def fill_edges(phase, scale, shift):
+        for way, (start, keep) in enumerate(((0, tile > 0), ((ROWS + 1) * W, tile < TILES - 1))):
+            for f in range(2):
+                value = jnp.concatenate(
+                    [
+                        halo[phase, way, 2 * f],
+                        halo[phase, way, 2 * f + 1],
+                        halo[phase, way, 4][:, f * 64 : (f + 1) * 64],
+                    ],
+                    axis=1,
+                )
+                put_taps(f, start, 1, value, scale[f : f + 1], shift[f : f + 1], keep)
+
+    def convolve(chunk, weights):
+        total = None
+        for a in range(3):
+            lines = [
+                taps[f, pl.ds((row + a) * W, W), :] for row in CHUNKS[chunk] for f in range(2)
+            ]
+            term = dot(jnp.concatenate(lines, axis=0), weights[a])
+            total = term if total is None else total + term
         return total
 
-    exchange_start(0, lat)
-    scale, shift = exchange_finish(0, lat, first, gain_one)
-    fill_taps(0, lat, scale, shift)
+    def first_convolution(chunk):
+        value = convolve(chunk, w_one).astype(BF16)
+        sums = []
+        for q, row in enumerate(CHUNKS[chunk]):
+            for f in range(2):
+                hid[f, pl.ds(row * W, W), :] = value[(2 * q + f) * W : (2 * q + f + 1) * W]
+        wide = value.astype(F32)
+        for f in range(2):
+            parts = [wide[(2 * q + f) * W : (2 * q + f + 1) * W] for q in range(len(CHUNKS[chunk]))]
+            sums.append(jnp.concatenate(parts, axis=0))
+        return channel_sums(sums)
+
+    stats_start(0)
+    halo_start(0)
+    scale, shift = stats_finish(0, first, gain_one)
+    fill_own(lat, scale, shift)
     loads[1].wait()
-    frames = []
-    for f in range(2):
-        value = convolve(f, 0, ROWS, w_one).astype(BF16)
-        hid[f] = value
-        frames.append(value.astype(F32))
-    second = channel_sums(frames)
+    second = first_convolution(0)
+    halo_finish(0)
+    fill_edges(0, scale, shift)
+    second = second + first_convolution(1)
     stat_send[1] = second
-
-    exchange_start(1, hid)
-    exchange_drain(0, lat)
-    scale, shift = exchange_finish(1, hid, second, gain_two)
-    fill_taps(1, hid, scale, shift)
+    pack_halo(1, hid)
+
+    stats_start(1)
+    halo_start(1)
+    exchange_drain(0)
     loads[2].wait()
+    scale, shift = stats_finish(1, second, gain_two)
+    fill_own(hid, scale, shift)
 
     def a2a_copy(way, chunk, source, target, peer, slot):
         return pltpu.make_async_remote_copy(
@@ -233,52 +271,67 @@
             [value[0:64, 256:320], value[64:128, 256:320]], axis=1
         )
 
+    def peer_at(i, sign):
+        block, place = lax.div(i, 8), lax.rem(i, 8)
+        mixed = lax.rem(i, 2)
+        outer = jnp.logical_or(block == 0, block == 3)
+        rest = jnp.where(outer, place, lax.div(i - 8, 2))
+        step_z = jnp.where(block == 0, 2, jnp.where(block == 3, 0, 1 + 2 * mixed))
+        turn = lax.div(rest, 2)
+        step_x = jnp.where(turn == 3, 0, jnp.where(turn == 2, 3, 2 - turn))
+        flip = 1 - lax.rem(rest, 2)
+        x, z, core = lax.div(clip, 8), lax.rem(lax.div(clip, 2), 4), lax.rem(clip, 2)
+        x = lax.rem(x + sign * step_x + 4, 4)
+        z = lax.rem(z + sign * step_z + 4, 4)
+        return (x * 4 + z) * 2 + lax.rem(core + flip, 2)
+
     def a2a_start(way, chunk, source, target):
-        row, rows = CHUNKS[chunk]
-        depth = rows * 10
+        depth = len(CHUNKS[chunk]) * 10
 
         def pick(peer):
-            return packed[pl.ds(row * 10 * CLIPS + peer, depth, stride=CLIPS), :].astype(BF16)
+            base = STARTS[chunk] * 10 * CLIPS
+            return packed[pl.ds(base + peer, depth, stride=CLIPS), :].astype(BF16)
 
         def stage(i, carry):
-            peer = lax.rem(clip + i, CLIPS)
+            peer = peer_at(i, 1)
             source[peer] = pick(peer)
             return carry
 
         def send(i, carry):
-            peer = lax.rem(clip + i, CLIPS)
+            peer = peer_at(i, 1)
             a2a_copy(way, chunk, source, target, peer, clip).start()
             return carry
 
-        lax.fori_loop(1, CLIPS, stage, 0)
+        lax.fori_loop(0, 8, stage, 0)
+        for block in range(3):
+            lax.fori_loop(block * 8 + 8, min(block * 8 + 16, 31), stage, 0)
+            lax.fori_loop(block * 8, block * 8 + 8, send, 0)
         target[clip] = pick(clip)
-        lax.fori_loop(1, CLIPS, send, 0)
+        lax.fori_loop(24, 31, send, 0)
 
     def a2a_finish(way, chunk, source, target):
-        rows = CHUNKS[chunk][1]
-        depth = rows * 10
+        depth = len(CHUNKS[chunk]) * 10
+
+        def widen(peer):
+            spread[pl.ds(pl.multiple_of(peer * 32, 32), depth), :] = target[peer].astype(F32)
 
         def arrive(i, carry):
-            peer = lax.rem(clip + i, CLIPS)
+            peer = peer_at(i, -1)
             a2a_copy(way, chunk, source, target, peer, peer).wait_recv()
-            return carry
-
-        lax.fori_loop(1, CLIPS, arrive, 0)
-
-        def widen(i, carry):
-            spread[pl.ds(pl.multiple_of(i * 32, 32), depth), :] = target[i].astype(F32)
-            return carry
-
-        lax.fori_loop(0, CLIPS, widen, 0)
-        return [unpack_row(q) for q in range(rows)]
+            widen(peer)
+            return carry
+
+        widen(clip)
+        lax.fori_loop(0, 31, arrive, 0)
+        return [unpack_row(q) for q in range(len(CHUNKS[chunk]))]
 
     def a2a_drain(way, chunk, source, target):
         def drain(i, carry):
-            peer = lax.rem(clip + i, CLIPS)
+            peer = peer_at(i, 1)
             a2a_copy(way, chunk, source, target, peer, clip).wait_send()
             return carry
 
-        lax.fori_loop(1, CLIPS, drain, 0)
+        lax.fori_loop(0, 31, drain, 0)
 
     def unpack_row(q):
         def column(k):
@@ -294,21 +347,23 @@
     sends, recvs = (send_0, send_1), (recv_0, recv_1)
     back_sends, back_recvs = (back_send_0, back_send_1), (back_recv_0, back_recv_1)
 
-    for chunk, (row, rows) in enumerate(CHUNKS):
-        halves = []
-        for f in range(2):
-            value = lat[f, pl.ds(row * W, rows * W), :].astype(F32) + convolve(f, row, rows, w_two)
-            if f == 1:
-                value = jnp.where(one_live, DEAD, value)
-            halves.append(value)
-        for q in range(rows):
-            span = slice(q * W, (q + 1) * W)
-            pack_row(row + q, jnp.concatenate([halves[0][span], halves[1][span]], axis=0))
+    for chunk in range(2):
+        if chunk == 1:
+            halo_finish(1)
+            fill_edges(1, scale, shift)
+        total = convolve(chunk, w_two)
+        for q, row in enumerate(CHUNKS[chunk]):
+            halves = []
+            for f in range(2):
+                span = slice((2 * q + f) * W, (2 * q + f + 1) * W)
+                value = lat[f, pl.ds(row * W, W), :].astype(F32) + total[span]
+                halves.append(jnp.where(one_live, DEAD, value) if f == 1 else value)
+            pack_row(STARTS[chunk] + q, jnp.concatenate(halves, axis=0))
         a2a_start(0, chunk, sends[chunk], recvs[chunk])
 
     for load in loads[3:]:
         load.wait()
-    exchange_drain(1, hid)
+    exchange_drain(1)
 
     lane = lax.broadcasted_iota(jnp.int32, (128, 128), 1)
     line = lax.broadcasted_iota(jnp.int32, (128, 128), 0)
@@ -321,7 +376,8 @@
     low_half = lane < HEAD_DIM
     clip_row = lax.broadcasted_iota(jnp.int32, (CLIPS, C), 0)
 
-    for chunk, (row, rows) in enumerate(CHUNKS):
+    for chunk in range(2):
+        rows = len(CHUNKS[chunk])
         blocks = a2a_finish(0, chunk, sends[chunk], recvs[chunk])
         dead = jnp.broadcast_to(blocks[0][64:96, 0:1], (CLIPS, 128)) > DEAD_LIMIT
         dead_wide = jnp.broadcast_to(blocks[0][64:96, 0:1], (CLIPS, C)) > DEAD_LIMIT
@@ -428,16 +484,16 @@
             parts = [block[0:64]]
             for cell in range(2):
                 parts.append(jnp.where(dead_wide, 0.0, block[64 + cell * 32 : 96 + cell * 32]))
-            pack_row(row + q, jnp.concatenate(parts, axis=0))
+            pack_row(STARTS[chunk] + q, jnp.concatenate(parts, axis=0))
         a2a_start(1, chunk, back_sends[chunk], back_recvs[chunk])
 
     for chunk in range(2):
         a2a_drain(0, chunk, sends[chunk], recvs[chunk])
-    for chunk, (row, rows) in enumerate(CHUNKS):
+    for chunk in range(2):
         blocks = a2a_finish(1, chunk, back_sends[chunk], back_recvs[chunk])
-        for q in range(rows):
+        for q, row in enumerate(CHUNKS[chunk]):
             for f in range(2):
-                out[f, pl.ds((row + q) * W, W), :] = blocks[q][f * 64 : (f + 1) * 64].astype(BF16)
+                out[f, pl.ds(row * W, W), :] = blocks[q][f * 64 : (f + 1) * 64].astype(BF16)
     for chunk in range(2):
         a2a_drain(1, chunk, back_sends[chunk], back_recvs[chunk])
 
@@ -451,7 +507,7 @@
     hbm = pl.BlockSpec(memory_space=pl.ANY)
 
     def messages(chunk):
-        return pltpu.VMEM((CLIPS, CHUNKS[chunk][1] * 10, 128), BF16)
+        return pltpu.VMEM((CLIPS, len(CHUNKS[chunk]) * 10, 128), BF16)
 
     result = pl.pallas_call(
         kernel,
@@ -467,9 +523,11 @@
             pltpu.VMEM((C, C), BF16),
             pltpu.VMEM((2, (ROWS + 2) * W, 3 * C), BF16),
             pltpu.VMEM((2, ROWS * W, C), BF16),
-            pltpu.VMEM((2, 2, 2, W, C), BF16),
-            pltpu.VMEM((2, 8, C), F32),
-            pltpu.VMEM((2, TILES, 8, C), F32),
+            pltpu.VMEM((2, 2, 5, W, 128), BF16),
+            pltpu.VMEM((2, 2, 5, W, 128), BF16),
+            pltpu.VMEM((C, C), BF16),
+            pltpu.VMEM((2, 4, C), F32),
+            pltpu.VMEM((2, TILES, 4, C), F32),
             pltpu.VMEM((ROWS * 10 * CLIPS, 128), F32),
             pltpu.VMEM((CLIPS * 32, 128), F32),
             messages(0), messages(1), messages(0), messages(1),

time: 67.1 us -> 62.5 us (0.931)
  Pallas kernels: 64.4 us -> 59.8 us
    pallas_call x1, Pallas kernels: 64.4 us -> 59.8 us  [local(): pl.pallas_call(kernel, out_shape=jax.ShapeDtypeStruct((2, ROWS * W, C), B...]
where the time goes in v3:
time: 62.5 us; the launch traced here: 62.3 us
  Pallas kernels  59.8 us (96%)
  local copies, waits for them, and re-layouts  1.86 us (3%)
  between operations  0.66 us (1%)
    pallas_call x1, Pallas kernels, local(): pl.pallas_call(kernel, out_shape=jax.ShapeDtypeStruct((2, ROWS * W, C), B...  59.8 us
    unnamed x1, local copies, waits for them, and re-layouts  1.86 us

profile of v3, /device:TPU:1, one launch (start us, length us, event | category | flops | bytes accessed | tf_op | source)
XLA Modules:
  0.0 62.3 jit_solution(8481349466764222176)
XLA Ops:
  0.7 59.8 %block.1 = bf16[2,320,320]{2,1,0:T(8,128)(2,1)} custom-call(bf16[2,320,320]{2,1,0:T(8,128)(2,1)} %bitcast.9, s32[1]{0:T(128)S(6)} %copy.13.length, s32[8]{0:T(128)} %context.1, f32[320]{0:T(512)} %gain_one.1, f32[320]{0:T(512)} %gain_two.1, f32[320]{0:T(512)} %gain_attn.1, bf16[3,960,320]{2,1,0:T(8,128)(2,1)} %bitcast.5, bf16[3,960,320]{2,1,0:T(8,128)(2,1)} %bitcast.6, ...), custom_call_target="tpu_custom_call" | custom-call | tf_op jit(solution)/shard_map/block/pallas_call | solution.py:512
  60.5 1.9 %copy.14 = bf16[2,5,64,320]{3,2,1,0:T(8,128)(2,1)} copy(bf16[2,5,64,320]{3,2,1,0:T(8,128)(2,1)} %bitcast.7) | data formatting | bytes 819200

commit v4 on v3

--- a/solution.py
+++ b/solution.py
@@ -27,6 +27,10 @@
 STARTS = (0, 3)
 
 
+def wrap(value, size):
+    return jnp.where(value >= size, value - size, value)
+
+
 def dot(a, b):
     return jnp.dot(a, b, preferred_element_type=F32)
 
@@ -47,10 +51,10 @@
 
 
 def kernel(
-    lat_hbm, length, context, gain_one, gain_two, gain_attn,
+    lat_hbm, length_hbm, context_hbm, gain_one_hbm, gain_two_hbm, gain_attn_hbm,
     w_one_hbm, w_two_hbm, w_time_hbm, w_qkv_hbm, w_out_hbm,
     out,
-    lat, w_one, w_two, w_time, w_qkv, w_out,
+    lat, length, context, gain_one, gain_two, gain_attn, w_one, w_two, w_time, w_qkv, w_out,
     taps, hid, halo_send, halo, member, stat_send, stat_recv, packed, spread,
     send_0, send_1, recv_0, recv_1, back_send_0, back_send_1, back_recv_0, back_recv_1,
     load_sem, halo_send_sem, halo_recv_sem, stat_send_sem, stat_recv_sem,
@@ -58,14 +62,18 @@
 ):
     clip = lax.axis_index("clip")
     tile = lax.axis_index("tile")
-    tile_up = lax.rem(tile + TILES - 1, TILES)
-    tile_down = lax.rem(tile + 1, TILES)
+    tile_up, tile_down = wrap(tile + TILES - 1, TILES), wrap(tile + 1, TILES)
 
     loads = [
         pltpu.make_async_copy(source, target, load_sem.at[i])
         for i, (source, target) in enumerate(
             (
                 (lat_hbm, lat),
+                (length_hbm, length),
+                (context_hbm, context),
+                (gain_one_hbm, gain_one),
+                (gain_two_hbm, gain_two),
+                (gain_attn_hbm, gain_attn),
                 (w_one_hbm, w_one),
                 (w_two_hbm, w_two),
                 (w_time_hbm, w_time),
@@ -79,20 +87,14 @@
 
     barrier = pltpu.get_barrier_semaphore()
 
-    def greet_tile(i, carry):
+    for i in range(1, CLIPS):
         pl.semaphore_signal(
-            barrier, inc=1, device_id={"tile": lax.rem(tile + i, TILES)}, device_id_type=MESH
-        )
-        return carry
-
-    def greet_clip(i, carry):
+            barrier, inc=1, device_id={"clip": wrap(clip + i, CLIPS)}, device_id_type=MESH
+        )
+    for i in range(1, TILES):
         pl.semaphore_signal(
-            barrier, inc=1, device_id={"clip": lax.rem(clip + i, CLIPS)}, device_id_type=MESH
-        )
-        return carry
-
-    lax.fori_loop(1, TILES, greet_tile, 0)
-    lax.fori_loop(1, CLIPS, greet_clip, 0)
+            barrier, inc=1, device_id={"tile": wrap(tile + i, TILES)}, device_id_type=MESH
+        )
 
     rows = lax.broadcasted_iota(jnp.int32, (C, C), 0)
     cols = lax.broadcasted_iota(jnp.int32, (C, C), 1)
@@ -108,7 +110,8 @@
                 [source[0, span, 256:320], source[1, span, 256:320]], axis=1
             )
 
-    loads[0].wait()
+    for load in loads[:6]:
+        load.wait()
     pack_halo(0, lat)
     first = channel_sums([lat[0].astype(F32), lat[1].astype(F32)])
     stat_send[0] = first
@@ -127,22 +130,20 @@
             for way, peer in enumerate((tile_down, tile_up))
         ]
 
-    def stat_copy(phase, peer, slot):
-        return pltpu.make_async_remote_copy(
-            src_ref=stat_send.at[phase],
-            dst_ref=stat_recv.at[phase, slot],
-            send_sem=stat_send_sem.at[phase, peer],
-            recv_sem=stat_recv_sem.at[phase, slot],
-            device_id={"tile": peer},
-            device_id_type=MESH,
-        )
-
     def stats_start(phase):
-        def send(i, carry):
-            stat_copy(phase, lax.rem(tile + i, TILES), tile).start()
-            return carry
-
-        lax.fori_loop(1, TILES, send, 0)
+        for i in range(1, TILES):
+            pltpu.make_async_remote_copy(
+                src_ref=stat_send.at[phase],
+                dst_ref=stat_recv.at[phase, tile],
+                send_sem=stat_send_sem.at[phase],
+                recv_sem=stat_recv_sem.at[phase],
+                device_id={"tile": wrap(tile + i, TILES)},
+                device_id_type=MESH,
+            ).start()
+
+    def batch_wait(buffer, count, sem):
+        span = buffer.at[pl.ds(0, count)]
+        pltpu.make_async_copy(span, span, sem).wait()
 
     def halo_start(phase):
         for copy in halo_copies(phase):
@@ -155,12 +156,7 @@
     def stats_finish(phase, own, gain):
         stat_recv[phase, tile] = own
 
-        def arrive(i, carry):
-            peer = lax.rem(tile + i, TILES)
-            stat_copy(phase, peer, peer).wait_recv()
-            return carry
-
-        lax.fori_loop(1, TILES, arrive, 0)
+        batch_wait(stat_recv.at[phase], TILES - 1, stat_recv_sem.at[phase])
         total = stat_recv[phase, 0]
         for i in range(1, TILES):
             total = total + stat_recv[phase, i]
@@ -176,11 +172,7 @@
         return scale, -centre * scale
 
     def exchange_drain(phase):
-        def drain(i, carry):
-            stat_copy(phase, lax.rem(tile + i, TILES), tile).wait_send()
-            return carry
-
-        lax.fori_loop(1, TILES, drain, 0)
+        batch_wait(stat_recv.at[phase], TILES - 1, stat_send_sem.at[phase])
         for copy in halo_copies(phase):
             copy.wait_send()
 
@@ -238,7 +230,7 @@
     halo_start(0)
     scale, shift = stats_finish(0, first, gain_one)
     fill_own(lat, scale, shift)
-    loads[1].wait()
+    loads[6].wait()
     second = first_convolution(0)
     halo_finish(0)
     fill_edges(0, scale, shift)
@@ -249,19 +241,9 @@
     stats_start(1)
     halo_start(1)
     exchange_drain(0)
-    loads[2].wait()
+    loads[7].wait()
     scale, shift = stats_finish(1, second, gain_two)
     fill_own(hid, scale, shift)
-
-    def a2a_copy(way, chunk, source, target, peer, slot):
-        return pltpu.make_async_remote_copy(
-            src_ref=source.at[peer],
-            dst_ref=target.at[slot],
-            send_sem=a2a_send_sem.at[way, chunk, peer],
-            recv_sem=a2a_recv_sem.at[way, chunk, slot],
-            device_id={"clip": peer},
-            device_id_type=MESH,
-        )
 
     def pack_row(r, value):
         base = r * 10 * CLIPS
@@ -271,67 +253,32 @@
             [value[0:64, 256:320], value[64:128, 256:320]], axis=1
         )
 
-    def peer_at(i, sign):
-        block, place = lax.div(i, 8), lax.rem(i, 8)
-        mixed = lax.rem(i, 2)
-        outer = jnp.logical_or(block == 0, block == 3)
-        rest = jnp.where(outer, place, lax.div(i - 8, 2))
-        step_z = jnp.where(block == 0, 2, jnp.where(block == 3, 0, 1 + 2 * mixed))
-        turn = lax.div(rest, 2)
-        step_x = jnp.where(turn == 3, 0, jnp.where(turn == 2, 3, 2 - turn))
-        flip = 1 - lax.rem(rest, 2)
-        x, z, core = lax.div(clip, 8), lax.rem(lax.div(clip, 2), 4), lax.rem(clip, 2)
-        x = lax.rem(x + sign * step_x + 4, 4)
-        z = lax.rem(z + sign * step_z + 4, 4)
-        return (x * 4 + z) * 2 + lax.rem(core + flip, 2)
-
     def a2a_start(way, chunk, source, target):
         depth = len(CHUNKS[chunk]) * 10
-
-        def pick(peer):
-            base = STARTS[chunk] * 10 * CLIPS
-            return packed[pl.ds(base + peer, depth, stride=CLIPS), :].astype(BF16)
-
-        def stage(i, carry):
-            peer = peer_at(i, 1)
-            source[peer] = pick(peer)
-            return carry
-
-        def send(i, carry):
-            peer = peer_at(i, 1)
-            a2a_copy(way, chunk, source, target, peer, clip).start()
-            return carry
-
-        lax.fori_loop(0, 8, stage, 0)
-        for block in range(3):
-            lax.fori_loop(block * 8 + 8, min(block * 8 + 16, 31), stage, 0)
-            lax.fori_loop(block * 8, block * 8 + 8, send, 0)
-        target[clip] = pick(clip)
-        lax.fori_loop(24, 31, send, 0)
+        base = STARTS[chunk] * 10 * CLIPS
+        for peer in range(CLIPS):
+            source[peer] = packed[pl.ds(base + peer, depth, stride=CLIPS), :].astype(BF16)
+        target[clip] = source[clip]
+        for i in range(1, CLIPS):
+            peer = wrap(clip + i, CLIPS)
+            pltpu.make_async_remote_copy(
+                src_ref=source.at[peer],
+                dst_ref=target.at[clip],
+                send_sem=a2a_send_sem.at[way, chunk],
+                recv_sem=a2a_recv_sem.at[way, chunk],
+                device_id={"clip": peer},
+                device_id_type=MESH,
+            ).start()
 
     def a2a_finish(way, chunk, source, target):
         depth = len(CHUNKS[chunk]) * 10
-
-        def widen(peer):
-            spread[pl.ds(pl.multiple_of(peer * 32, 32), depth), :] = target[peer].astype(F32)
-
-        def arrive(i, carry):
-            peer = peer_at(i, -1)
-            a2a_copy(way, chunk, source, target, peer, peer).wait_recv()
-            widen(peer)
-            return carry
-
-        widen(clip)
-        lax.fori_loop(0, 31, arrive, 0)
+        batch_wait(target, CLIPS - 1, a2a_recv_sem.at[way, chunk])
+        for peer in range(CLIPS):
+            spread[pl.ds(peer * 32, depth), :] = target[peer].astype(F32)
         return [unpack_row(q) for q in range(len(CHUNKS[chunk]))]
 
     def a2a_drain(way, chunk, source, target):
-        def drain(i, carry):
-            peer = peer_at(i, 1)
-            a2a_copy(way, chunk, source, target, peer, clip).wait_send()
-            return carry
-
-        lax.fori_loop(0, 31, drain, 0)
+        batch_wait(source, CLIPS - 1, a2a_send_sem.at[way, chunk])
 
     def unpack_row(q):
         def column(k):
@@ -361,7 +308,7 @@
             pack_row(STARTS[chunk] + q, jnp.concatenate(halves, axis=0))
         a2a_start(0, chunk, sends[chunk], recvs[chunk])
 
-    for load in loads[3:]:
+    for load in loads[8:]:
         load.wait()
     exchange_drain(1)
 
@@ -503,8 +450,7 @@
     time_weight, attn_gain, w_qkv, w_out,
 ):
     vmem = pl.BlockSpec(memory_space=pltpu.VMEM)
-    smem = pl.BlockSpec(memory_space=pltpu.SMEM)
-    hbm = pl.BlockSpec(memory_space=pl.ANY)
+    hbm = pl.BlockSpec(memory_space=pltpu.HBM)
 
     def messages(chunk):
         return pltpu.VMEM((CLIPS, len(CHUNKS[chunk]) * 10, 128), BF16)
@@ -512,10 +458,15 @@
     result = pl.pallas_call(
         kernel,
         out_shape=jax.ShapeDtypeStruct((2, ROWS * W, C), BF16),
-        in_specs=[hbm, smem, smem, vmem, vmem, vmem, hbm, hbm, hbm, hbm, hbm],
+        in_specs=[hbm] * 11,
         out_specs=vmem,
         scratch_shapes=[
             pltpu.VMEM((2, ROWS * W, C), BF16),
+            pltpu.SMEM((1,), jnp.int32),
+            pltpu.SMEM((8,), jnp.int32),
+            pltpu.VMEM((C,), F32),
+            pltpu.VMEM((C,), F32),
+            pltpu.VMEM((C,), F32),
             pltpu.VMEM((3, 3 * C, C), BF16),
             pltpu.VMEM((3, 3 * C, C), BF16),
             pltpu.VMEM((3 * C, C), BF16),
@@ -532,16 +483,16 @@
             pltpu.VMEM((CLIPS * 32, 128), F32),
             messages(0), messages(1), messages(0), messages(1),
             messages(0), messages(1), messages(0), messages(1),
-            pltpu.SemaphoreType.DMA((6,)),
+            pltpu.SemaphoreType.DMA((11,)),
             pltpu.SemaphoreType.DMA((2, 2)),
             pltpu.SemaphoreType.DMA((2, 2)),
-            pltpu.SemaphoreType.DMA((2, TILES)),
-            pltpu.SemaphoreType.DMA((2, TILES)),
-            pltpu.SemaphoreType.DMA((2, 2, CLIPS)),
-            pltpu.SemaphoreType.DMA((2, 2, CLIPS)),
+            pltpu.SemaphoreType.DMA((2,)),
+            pltpu.SemaphoreType.DMA((2,)),
+            pltpu.SemaphoreType.DMA((2, 2)),
+            pltpu.SemaphoreType.DMA((2, 2)),
         ],
         compiler_params=pltpu.CompilerParams(
-            collective_id=0, has_side_effects=True, vmem_limit_bytes=67043328
+            collective_id=0, has_side_effects=True, vmem_limit_bytes=56 << 20
         ),
         name="block",
     )(

time: 62.5 us -> 55.8 us (0.89)
  Pallas kernels: 59.8 us -> 53.1 us
    pallas_call x1, Pallas kernels: 59.8 us -> 53.1 us  [local(): pl.pallas_call(kernel, out_shape=jax.ShapeDtypeStruct((2, ROWS * W, C), B...]
where the time goes in v4:
time: 55.8 us; the launch traced here: 55.7 us
  Pallas kernels  53.1 us (95%)
  local copies, waits for them, and re-layouts  1.86 us (3%)
  between operations  0.66 us (1%)
    pallas_call x1, Pallas kernels, local(): pl.pallas_call(kernel, out_shape=jax.ShapeDtypeStruct((2, ROWS * W, C), B...  53.1 us
    unnamed x1, local copies, waits for them, and re-layouts  1.86 us

profile of v4, /device:TPU:1, one launch (start us, length us, event | category | flops | bytes accessed | tf_op | source)
XLA Modules:
  0.0 55.7 jit_solution(3700758924155087419)
XLA Ops:
  0.7 53.1 %block.1 = bf16[2,320,320]{2,1,0:T(8,128)(2,1)} custom-call(bf16[2,320,320]{2,1,0:T(8,128)(2,1)} %bitcast.9, s32[1]{0:T(128)S(6)} %copy.13.length_hbm, s32[8]{0:T(128)} %context_hbm.1, f32[320]{0:T(512)} %gain_one_hbm.1, f32[320]{0:T(512)} %gain_two_hbm.1, f32[320]{0:T(512)} %gain_attn_hbm.1, bf16[3,960,320]{2,1,0:T(8,128)(2,1)} %bitcast.5, ...), custom_call_target="tpu_custom_call" | custom-call | tf_op jit(solution)/shard_map/block/pallas_call | solution.py:458
  53.8 1.9 %copy.14 = bf16[2,5,64,320]{3,2,1,0:T(8,128)(2,1)} copy(bf16[2,5,64,320]{3,2,1,0:T(8,128)(2,1)} %bitcast.7) | data formatting | bytes 819200

commit v5 on v4

--- a/solution.py
+++ b/solution.py
@@ -445,6 +445,10 @@
         a2a_drain(1, chunk, back_sends[chunk], back_recvs[chunk])
 
 
+def in_hbm(x):
+    return pltpu.with_memory_space_constraint(x, pltpu.HBM)
+
+
 def local(
     latents, lengths, context, gain_first, conv_first, gain_second, conv_second,
     time_weight, attn_gain, w_qkv, w_out,
@@ -492,21 +496,21 @@
             pltpu.SemaphoreType.DMA((2, 2)),
         ],
         compiler_params=pltpu.CompilerParams(
-            collective_id=0, has_side_effects=True, vmem_limit_bytes=56 << 20
+            collective_id=0, has_side_effects=True, vmem_limit_bytes=48 << 20
         ),
         name="block",
     )(
-        latents.reshape(2, ROWS * W, C),
+        in_hbm(latents.reshape(2, ROWS * W, C)),
         lengths,
-        context,
-        gain_first,
-        gain_second,
-        attn_gain,
-        conv_first.reshape(3, 3 * C, C),
-        conv_second.reshape(3, 3 * C, C),
-        time_weight.reshape(3 * C, C),
-        w_qkv,
-        w_out,
+        in_hbm(context),
+        in_hbm(gain_first),
+        in_hbm(gain_second),
+        in_hbm(attn_gain),
+        in_hbm(conv_first.reshape(3, 3 * C, C)),
+        in_hbm(conv_second.reshape(3, 3 * C, C)),
+        in_hbm(time_weight.reshape(3 * C, C)),
+        in_hbm(w_qkv),
+        in_hbm(w_out),
     )
     return result.reshape(2, ROWS, W, C)
 

time: 55.8 us -> 53.9 us (0.966)
  local copies, waits for them, and re-layouts: 1.86 us -> 0.78 us
  Pallas kernels: 53.1 us -> 52.4 us
    unnamed x1, local copies, waits for them, and re-layouts: 1.86 us -> 0.78 us
    pallas_call x1, Pallas kernels: 53.1 us -> 52.4 us  [local(): pl.pallas_call(kernel, out_shape=jax.ShapeDtypeStruct((2, ROWS * W, C), B...]
where the time goes in v5:
time: 53.9 us; the launch traced here: 53.8 us
  Pallas kernels  52.4 us (97%)
  local copies, waits for them, and re-layouts  0.78 us (1%)
  between operations  0.66 us (1%)
    pallas_call x1, Pallas kernels, local(): pl.pallas_call(kernel, out_shape=jax.ShapeDtypeStruct((2, ROWS * W, C), B...  52.4 us

profile of v5, /device:TPU:1, one launch (start us, length us, event | category | flops | bytes accessed | tf_op | source)
XLA Modules:
  0.0 53.8 jit_solution(12850841252222154625)
XLA Ops:
  0.7 52.4 %block.1 = bf16[2,320,320]{2,1,0:T(8,128)(2,1)S(1)} custom-call(bf16[2,320,320]{2,1,0:T(8,128)(2,1)} %bitcast.9, s32[1]{0:T(128)S(6)} %copy.13.length_hbm, s32[8]{0:T(128)} %context_hbm.1, f32[320]{0:T(512)} %gain_one_hbm.1, f32[320]{0:T(512)} %gain_two_hbm.1, f32[320]{0:T(512)} %gain_attn_hbm.1, bf16[3,960,320]{2,1,0:T(8,128)(2,1)} %bitcast.6, ...), custom_call_target="tpu_custom_call" | custom-call | tf_op jit(solution)/shard_map/block/pallas_call | solution.py:462
  53.0 0.8 %copy.14 = bf16[2,5,64,320]{3,2,1,0:T(8,128)(2,1)} copy(bf16[2,5,64,320]{3,2,1,0:T(8,128)(2,1)S(1)} %bitcast.5) | data formatting | bytes 819200

commit v6 on v5

--- a/solution.py
+++ b/solution.py
@@ -55,7 +55,7 @@
     w_one_hbm, w_two_hbm, w_time_hbm, w_qkv_hbm, w_out_hbm,
     out,
     lat, length, context, gain_one, gain_two, gain_attn, w_one, w_two, w_time, w_qkv, w_out,
-    taps, hid, halo_send, halo, member, stat_send, stat_recv, packed, spread,
+    taps, hid, halo_send, halo, member, stat_send, stat_recv, packed, qkv, masks,
     send_0, send_1, recv_0, recv_1, back_send_0, back_send_1, back_recv_0, back_recv_1,
     load_sem, halo_send_sem, halo_recv_sem, stat_send_sem, stat_recv_sem,
     a2a_send_sem, a2a_recv_sem,
@@ -228,9 +228,12 @@
 
     stats_start(0)
     halo_start(0)
+    for load in loads[6:]:
+        load.wait()
+    for i in range(3):
+        qkv[i] = w_qkv[:, i * C : (i + 1) * C]
     scale, shift = stats_finish(0, first, gain_one)
     fill_own(lat, scale, shift)
-    loads[6].wait()
     second = first_convolution(0)
     halo_finish(0)
     fill_edges(0, scale, shift)
@@ -241,7 +244,6 @@
     stats_start(1)
     halo_start(1)
     exchange_drain(0)
-    loads[7].wait()
     scale, shift = stats_finish(1, second, gain_two)
     fill_own(hid, scale, shift)
 
@@ -256,8 +258,8 @@
     def a2a_start(way, chunk, source, target):
         depth = len(CHUNKS[chunk]) * 10
         base = STARTS[chunk] * 10 * CLIPS
-        for peer in range(CLIPS):
-            source[peer] = packed[pl.ds(base + peer, depth, stride=CLIPS), :].astype(BF16)
+        block = packed[pl.ds(base, depth * CLIPS), :].reshape(depth, CLIPS, 128)
+        source[...] = jnp.swapaxes(block, 0, 1).astype(BF16)
         target[clip] = source[clip]
         for i in range(1, CLIPS):
             peer = wrap(clip + i, CLIPS)
@@ -271,22 +273,16 @@
             ).start()
 
     def a2a_finish(way, chunk, source, target):
-        depth = len(CHUNKS[chunk]) * 10
         batch_wait(target, CLIPS - 1, a2a_recv_sem.at[way, chunk])
-        for peer in range(CLIPS):
-            spread[pl.ds(peer * 32, depth), :] = target[peer].astype(F32)
-        return [unpack_row(q) for q in range(len(CHUNKS[chunk]))]
+        block = jnp.swapaxes(target[...].astype(F32), 0, 1)
+        return [unpack_row(block[q * 10 : q * 10 + 10]) for q in range(len(CHUNKS[chunk]))]
 
     def a2a_drain(way, chunk, source, target):
         batch_wait(source, CLIPS - 1, a2a_send_sem.at[way, chunk])
 
-    def unpack_row(q):
-        def column(k):
-            return spread[pl.ds(q * 10 + k, CLIPS, stride=32), :]
-
-        left = jnp.concatenate([column(k) for k in range(4)], axis=0)
-        middle = jnp.concatenate([column(4 + k) for k in range(4)], axis=0)
-        tail = jnp.concatenate([column(8), column(9)], axis=0)
+    def unpack_row(block):
+        left, middle = block[0:4].reshape(128, 128), block[4:8].reshape(128, 128)
+        tail = block[8:10].reshape(64, 128)
         right = jnp.concatenate([tail, pltpu.roll(tail, 64, 1)], axis=0)
         return jnp.concatenate([left, middle, right[:, 0:64]], axis=1)
 
@@ -308,8 +304,6 @@
             pack_row(STARTS[chunk] + q, jnp.concatenate(halves, axis=0))
         a2a_start(0, chunk, sends[chunk], recvs[chunk])
 
-    for load in loads[8:]:
-        load.wait()
     exchange_drain(1)
 
     lane = lax.broadcasted_iota(jnp.int32, (128, 128), 1)
@@ -326,28 +320,28 @@
     for chunk in range(2):
         rows = len(CHUNKS[chunk])
         blocks = a2a_finish(0, chunk, sends[chunk], recvs[chunk])
-        dead = jnp.broadcast_to(blocks[0][64:96, 0:1], (CLIPS, 128)) > DEAD_LIMIT
-        dead_wide = jnp.broadcast_to(blocks[0][64:96, 0:1], (CLIPS, C)) > DEAD_LIMIT
-        dead_f = jnp.where(dead, 1.0, 0.0)
-        dead_lane = jnp.sum(
-            jnp.where(
-                lax.broadcasted_iota(jnp.int32, (CLIPS, 128), 0)
-                == (lax.broadcasted_iota(jnp.int32, (CLIPS, 128), 1) & 31),
-                dead_f,
+        if chunk == 0:
+            dead = jnp.broadcast_to(blocks[0][64:96, 0:1], (CLIPS, 128)) > DEAD_LIMIT
+            dead_wide = jnp.broadcast_to(blocks[0][64:96, 0:1], (CLIPS, C)) > DEAD_LIMIT
+            dead_f = jnp.where(dead, 1.0, 0.0)
+            dead_lane = jnp.sum(
+                jnp.where(
+                    lax.broadcasted_iota(jnp.int32, (CLIPS, 128), 0)
+                    == (lax.broadcasted_iota(jnp.int32, (CLIPS, 128), 1) & 31),
+                    dead_f,
+                    0.0,
+                ),
+                axis=0,
+                keepdims=True,
+            )
+            live_key = 1.0 - jnp.where(lane_slot == 1, jnp.broadcast_to(dead_lane, (128, 128)), 0.0)
+            weight = jnp.where(
+                lane_cell == line_cell,
+                jnp.where(lane_clip == line_clip, live_key, 0.0) + shared,
                 0.0,
-            ),
-            axis=0,
-            keepdims=True,
-        )
-        live_key = 1.0 - jnp.where(lane_slot == 1, jnp.broadcast_to(dead_lane, (128, 128)), 0.0)
-        weight = jnp.where(
-            lane_cell == line_cell,
-            jnp.where(lane_clip == line_clip, live_key, 0.0) + shared,
-            0.0,
-        )
-        visible = weight > 0.0
-        weight2 = jnp.concatenate([weight, weight], axis=1)
-        visible2 = jnp.concatenate([visible, visible], axis=1)
+            )
+            masks[0] = weight
+            masks[1] = jnp.where(weight > 0.0, 0.0, MASKED)
 
         sources = []
         for q in range(rows):
@@ -377,9 +371,9 @@
         offset = res_two - centre
         variance = jnp.mean(offset * offset, axis=1, keepdims=True)
         normed = (offset * lax.rsqrt(variance + EPS) * gain_attn[...].reshape(1, C)).astype(BF16)
-        q_all = dot(normed, w_qkv[:, 0:C]).astype(BF16)
-        k_all = dot(normed, w_qkv[:, C : 2 * C]).astype(BF16)
-        v_all = dot(normed, w_qkv[:, 2 * C : 3 * C]).astype(BF16)
+        q_all = (dot(normed, qkv[0]) * (HEAD_DIM**-0.5)).astype(BF16)
+        k_all = dot(normed, qkv[1]).astype(BF16)
+        v_all = dot(normed, qkv[2]).astype(BF16)
         zero = jnp.zeros((128, 128), BF16)
         attended = []
         for q in range(rows):
@@ -396,32 +390,23 @@
                 )
                 scores = lax.dot_general(
                     queries, keys2, (((1,), (1,)), ((), ())), preferred_element_type=F32
-                ) * (HEAD_DIM**-0.5)
-                scores = jnp.where(visible2, scores, MASKED)
-                top = jnp.concatenate(
-                    [
-                        jnp.broadcast_to(
-                            jnp.max(scores[:, i * 128 : (i + 1) * 128], axis=1, keepdims=True),
-                            (128, 128),
-                        )
-                        for i in range(2)
-                    ],
-                    axis=1,
                 )
-                grown = jnp.exp(scores - top) * weight2
-                norm = jnp.where(
-                    low_half,
-                    jnp.broadcast_to(jnp.sum(grown[:, 0:128], axis=1, keepdims=True), (128, 128)),
-                    jnp.broadcast_to(jnp.sum(grown[:, 128:256], axis=1, keepdims=True), (128, 128)),
-                )
-                pieces.append((dot(grown.astype(BF16), values2) / norm).astype(BF16))
+                grown, norms = [], []
+                for i in range(2):
+                    part = scores[:, i * 128 : (i + 1) * 128] + masks[1]
+                    part = jnp.exp(part - jnp.max(part, axis=1, keepdims=True)) * masks[0]
+                    norms.append(jnp.broadcast_to(jnp.sum(part, axis=1, keepdims=True), (128, 128)))
+                    grown.append(part.astype(BF16))
+                norm = jnp.where(low_half, norms[0], norms[1])
+                grown = jnp.concatenate(grown, axis=1)
+                pieces.append((dot(grown, values2) / norm).astype(BF16))
             cols = slice(256, 320)
             scores = lax.dot_general(
                 q_all[span, cols], k_all[span, cols], (((1,), (1,)), ((), ())),
                 preferred_element_type=F32,
-            ) * (HEAD_DIM**-0.5)
-            scores = jnp.where(visible, scores, MASKED)
-            grown = jnp.exp(scores - jnp.max(scores, axis=1, keepdims=True)) * weight
+            )
+            scores = scores + masks[1]
+            grown = jnp.exp(scores - jnp.max(scores, axis=1, keepdims=True)) * masks[0]
             norm = jnp.sum(grown, axis=1, keepdims=True)
             pieces.append((dot(grown.astype(BF16), v_all[span, cols]) / norm).astype(BF16))
             attended.append(jnp.concatenate(pieces, axis=1))
@@ -484,7 +469,8 @@
             pltpu.VMEM((2, 4, C), F32),
             pltpu.VMEM((2, TILES, 4, C), F32),
             pltpu.VMEM((ROWS * 10 * CLIPS, 128), F32),
-            pltpu.VMEM((CLIPS * 32, 128), F32),
+            pltpu.VMEM((3, C, C), BF16),
+            pltpu.VMEM((2, 128, 128), F32),
             messages(0), messages(1), messages(0), messages(1),
             messages(0), messages(1), messages(0), messages(1),
             pltpu.SemaphoreType.DMA((11,)),

time: 53.9 us -> 52.8 us (0.980)
  Pallas kernels: 52.4 us -> 51.3 us
    pallas_call x1, Pallas kernels: 52.4 us -> 51.3 us  [local(): pl.pallas_call(kernel, out_shape=jax.ShapeDtypeStruct((2, ROWS * W, C), B...]
where the time goes in v6:
time: 52.8 us; the launch traced here: 52.7 us
  Pallas kernels  51.3 us (97%)
  local copies, waits for them, and re-layouts  0.78 us (1%)
  between operations  0.66 us (1%)
    pallas_call x1, Pallas kernels, local(): pl.pallas_call(kernel, out_shape=jax.ShapeDtypeStruct((2, ROWS * W, C), B...  51.3 us

profile of v6, /device:TPU:1, one launch (start us, length us, event | category | flops | bytes accessed | tf_op | source)
XLA Modules:
  0.0 52.7 jit_solution(12540695278165783768)
XLA Ops:
  0.7 51.3 %block.1 = bf16[2,320,320]{2,1,0:T(8,128)(2,1)S(1)} custom-call(bf16[2,320,320]{2,1,0:T(8,128)(2,1)} %bitcast.9, s32[1]{0:T(128)S(6)} %copy.13.length_hbm, s32[8]{0:T(128)} %context_hbm.1, f32[320]{0:T(512)} %gain_one_hbm.1, f32[320]{0:T(512)} %gain_two_hbm.1, f32[320]{0:T(512)} %gain_attn_hbm.1, bf16[3,960,320]{2,1,0:T(8,128)(2,1)} %bitcast.6, ...), custom_call_target="tpu_custom_call" | custom-call | tf_op jit(solution)/shard_map/block/pallas_call | solution.py:447
  52.0 0.8 %copy.14 = bf16[2,5,64,320]{3,2,1,0:T(8,128)(2,1)} copy(bf16[2,5,64,320]{3,2,1,0:T(8,128)(2,1)S(1)} %bitcast.5) | data formatting | bytes 819200

commit v7 on v6

--- a/solution.py
+++ b/solution.py
@@ -23,8 +23,8 @@
 MASKED = -1e30
 DEAD = 1e30
 DEAD_LIMIT = 1e20
-CHUNKS = ((1, 2, 3), (0, 4))
-STARTS = (0, 3)
+CHUNKS = ((1, 2), (3, 0, 4))
+STARTS = (0, 2)
 
 
 def wrap(value, size):

time: 52.8 us -> 51.9 us (0.983)
  Pallas kernels: 51.3 us -> 50.4 us
    pallas_call x1, Pallas kernels: 51.3 us -> 50.4 us  [local(): pl.pallas_call(kernel, out_shape=jax.ShapeDtypeStruct((2, ROWS * W, C), B...]
where the time goes in v7:
time: 51.9 us
  Pallas kernels  50.4 us (97%)
  local copies, waits for them, and re-layouts  0.78 us (2%)
  between operations  0.66 us (1%)
    pallas_call x1, Pallas kernels, local(): pl.pallas_call(kernel, out_shape=jax.ShapeDtypeStruct((2, ROWS * W, C), B...  50.4 us

profile of v7, /device:TPU:1, one launch (start us, length us, event | category | flops | bytes accessed | tf_op | source)
XLA Modules:
  0.0 51.9 jit_solution(17260204439278900194)
XLA Ops:
  0.7 50.4 %block.1 = bf16[2,320,320]{2,1,0:T(8,128)(2,1)S(1)} custom-call(bf16[2,320,320]{2,1,0:T(8,128)(2,1)} %bitcast.9, s32[1]{0:T(128)S(6)} %copy.13.length_hbm, s32[8]{0:T(128)} %context_hbm.1, f32[320]{0:T(512)} %gain_one_hbm.1, f32[320]{0:T(512)} %gain_two_hbm.1, f32[320]{0:T(512)} %gain_attn_hbm.1, bf16[3,960,320]{2,1,0:T(8,128)(2,1)} %bitcast.6, ...), custom_call_target="tpu_custom_call" | custom-call | tf_op jit(solution)/shard_map/block/pallas_call | solution.py:447
  51.1 0.8 %copy.14 = bf16[2,5,64,320]{3,2,1,0:T(8,128)(2,1)} copy(bf16[2,5,64,320]{3,2,1,0:T(8,128)(2,1)S(1)} %bitcast.5) | data formatting | bytes 819200

commit v8 on v7

--- a/solution.py
+++ b/solution.py
@@ -259,7 +259,7 @@
         depth = len(CHUNKS[chunk]) * 10
         base = STARTS[chunk] * 10 * CLIPS
         block = packed[pl.ds(base, depth * CLIPS), :].reshape(depth, CLIPS, 128)
-        source[...] = jnp.swapaxes(block, 0, 1).astype(BF16)
+        source[...] = jnp.swapaxes(block, 0, 1).astype(BF16).reshape(CLIPS, depth // 2, 2, 128)
         target[clip] = source[clip]
         for i in range(1, CLIPS):
             peer = wrap(clip + i, CLIPS)
@@ -274,7 +274,8 @@
 
     def a2a_finish(way, chunk, source, target):
         batch_wait(target, CLIPS - 1, a2a_recv_sem.at[way, chunk])
-        block = jnp.swapaxes(target[...].astype(F32), 0, 1)
+        wide = target[...].reshape(CLIPS, len(CHUNKS[chunk]) * 10, 128).astype(F32)
+        block = jnp.swapaxes(wide, 0, 1)
         return [unpack_row(block[q * 10 : q * 10 + 10]) for q in range(len(CHUNKS[chunk]))]
 
     def a2a_drain(way, chunk, source, target):
@@ -442,7 +443,7 @@
     hbm = pl.BlockSpec(memory_space=pltpu.HBM)
 
     def messages(chunk):
-        return pltpu.VMEM((CLIPS, len(CHUNKS[chunk]) * 10, 128), BF16)
+        return pltpu.VMEM((CLIPS, len(CHUNKS[chunk]) * 5, 2, 128), BF16)
 
     result = pl.pallas_call(
         kernel,

time: 51.9 us -> 50.9 us (0.981)
  Pallas kernels: 50.4 us -> 49.3 us
    pallas_call x1, Pallas kernels: 50.4 us -> 49.3 us  [local(): pl.pallas_call(kernel, out_shape=jax.ShapeDtypeStruct((2, ROWS * W, C), B...]
where the time goes in v8:
time: 50.9 us; the launch traced here: 50.8 us
  Pallas kernels  49.3 us (97%)
  local copies, waits for them, and re-layouts  0.78 us (2%)
  between operations  0.66 us (1%)
    pallas_call x1, Pallas kernels, local(): pl.pallas_call(kernel, out_shape=jax.ShapeDtypeStruct((2, ROWS * W, C), B...  49.3 us

profile of v8, /device:TPU:1, one launch (start us, length us, event | category | flops | bytes accessed | tf_op | source)
XLA Modules:
  0.0 50.8 jit_solution(5031391325128938023)
XLA Ops:
  0.7 49.3 %block.1 = bf16[2,320,320]{2,1,0:T(8,128)(2,1)S(1)} custom-call(bf16[2,320,320]{2,1,0:T(8,128)(2,1)} %bitcast.9, s32[1]{0:T(128)S(6)} %copy.13.length_hbm, s32[8]{0:T(128)} %context_hbm.1, f32[320]{0:T(512)} %gain_one_hbm.1, f32[320]{0:T(512)} %gain_two_hbm.1, f32[320]{0:T(512)} %gain_attn_hbm.1, bf16[3,960,320]{2,1,0:T(8,128)(2,1)} %bitcast.6, ...), custom_call_target="tpu_custom_call" | custom-call | tf_op jit(solution)/shard_map/block/pallas_call | solution.py:448
  50.0 0.8 %copy.14 = bf16[2,5,64,320]{3,2,1,0:T(8,128)(2,1)} copy(bf16[2,5,64,320]{3,2,1,0:T(8,128)(2,1)S(1)} %bitcast.5) | data formatting | bytes 819200
